TPU v7x, 256 devices: a whole 4x4x8 slice. The times are simulated.
256 devices in a mesh: state: 32 (over x, y, z_lo), group: 8 (over z_hi, core).
Axes of the slice: x: 4, y: 4, z: 8 (z_hi: 4, z_lo: 2; z = z_hi * 2 + z_lo), core: 2. Of those that a mesh axis runs over, the one named last changes fastest.
Arguments:
- basis_rows: bfloat16 [98304, 512], P('state'), may hold values from -6 to 6
- tile_blocks: bfloat16 [32, 8, 32, 6, 128, 128], P('state', 'group'), may hold values from -0.09375 to 0.09375
- tile_cols: int32 [32, 8, 32], P('state', 'group'), may hold values from 0 to 23
- tile_rows: int32 [32, 8, 32, 6], P('state', 'group'), may hold values from 0 to 23, as said below
- tile_counts: int32 [32, 8, 32], P('state', 'group'), may hold values from 1 to 6, as said below
Outputs:
- coupling: float32 [512, 512], P(('state', 'group'))
Inputs may be any that keep to these rules, and one draw needn't show every extreme that they name: `tile_rows`: the 6 block-rows of one (s, g, p) are distinct. `tile_counts`: on every device some source shard has all 6 slots live.
All inputs are finite; a program needn't handle non-finite values.
Results may differ from a plain program's by a relative error of at most 0.0003.
Values may be sent and summed in bfloat16 or wider, within the bound.
No kernel may reach another device: no remote copies, remote signals or barrier semaphores. Data moves between devices by JAX's collectives and lax.ppermute only.
A program may use at most 128 MiB of HBM per device.

v0:
```python
import math

import jax
import jax.numpy as jnp
from jax import lax
from jax.sharding import PartitionSpec as P

discount = 0.95


def split_pair(values):
    high_part = lax.optimization_barrier(values.astype(jnp.bfloat16))
    low_part = (values - high_part.astype(jnp.float32)).astype(jnp.bfloat16)
    return (high_part, low_part)


def body(basis_rows, tile_blocks, tile_cols, tile_rows, tile_counts):
    shards = lax.axis_size("state")
    local_rows = basis_rows.shape[0]
    feature_count = basis_rows.shape[1]
    tile_size = tile_blocks.shape[-1]
    block_count = local_rows // tile_size
    use_count = tile_blocks.shape[3]
    blocks = basis_rows.reshape(block_count, tile_size, feature_count)
    wanted_cols = tile_cols[0, 0]
    target_rows = tile_rows[0, 0]
    live_mask = jnp.arange(use_count, dtype=jnp.int32)[None, :] < tile_counts[0, 0][:, None]
    tile_set = jnp.where(
        live_mask[:, :, None, None], tile_blocks[0, 0], jnp.zeros((), jnp.bfloat16)
    )
    owner_first = (lax.axis_index("group") == 0).astype(jnp.float32)
    asked_cols = lax.all_to_all(wanted_cols, "state", split_axis=0, concat_axis=0, tiled=True)
    outgoing = blocks[asked_cols]
    received = lax.all_to_all(outgoing, "state", split_axis=0, concat_axis=0, tiled=True)
    running = jnp.zeros((block_count, tile_size, received.shape[2]), jnp.float32)
    for which in range(use_count):
        product = jnp.einsum(
            "pij,pjk->pik", tile_set[:, which], received, preferred_element_type=jnp.float32
        )
        running = running.at[target_rows[:, which]].add(product)
    residual = owner_first * basis_rows.astype(jnp.float32) - discount * running.reshape(
        local_rows, feature_count
    )
    residual_high, residual_low = split_pair(residual)
    upper = jnp.dot(basis_rows.T, residual_high, preferred_element_type=jnp.float32)
    summed = lax.psum_scatter(
        upper + jnp.dot(basis_rows.T, residual_low, preferred_element_type=jnp.float32),
        ("state", "group"),
        scatter_dimension=0,
        tiled=True,
    )
    return summed * (1.0 / math.sqrt(local_rows * shards))


def solution(mesh):
    in_specs = (
        P("state", None),
        P("state", "group", None, None, None, None),
        P("state", "group", None),
        P("state", "group", None, None),
        P("state", "group", None),
    )
    out_specs = P(("state", "group"), None)
    return jax.shard_map(body, mesh=mesh, in_specs=in_specs, out_specs=out_specs, check_vma=False)
```

profile of v0, /device:TPU:1, one launch (start us, length us, event | category | flops | bytes accessed | tf_op | source)
XLA Modules:
  0.0 529.3 jit_solution(6199467435582917657)
XLA Ops:
  6.5 0.7 copy.15
  7.3 16.1 %all_to_all.17 = s32[32,1,1]{2,1,0:T(1,128)S(1)} all-to-all(s32[32,1,1]{2,1,0:T(1,128)S(1)} %copy.15), channel_id=1, replica_groups=mesh['state'=32,'group'=8] {'state'}, dimensions={0} | all-to-all | bytes 256 | tf_op jit(solution)/shard_map/all_to_all | solution.py:32
  23.4 0.7 reduce
  24.1 4.7 gather_fusion
  28.8 5.0 all-to-all-start.1
  33.7 0.0 all-reduce.3.cloned.1.call-start
  33.8 0.0 copy-done.1
  33.9 6.6 %bitcast_select_fusion = bf16[32,6,128,128]{3,2,0,1:T(8,128)(2,1)} fusion(bf16[1,1,32,6,128,128]{5,4,3,2,1,0:T(8,128)(2,1)} %param.6, pred[32,6]{0,1:T(8,128)(4,1)S(1)} %iota_compare_fusion), kind=kLoop, calls=%fused_computation.8 | loop fusion | flops 3145728 | bytes 12583104 | tf_op jit(solution)/shard_map/jit(_where)/select_n | solution.py:28
  40.5 54.4 %all-to-all-done.1 = bf16[32,128,512]{2,1,0:T(8,128)(2,1)} async-done(((bf16[32,128,512]{2,1,0:T(8,128)(2,1)}), bf16[32,128,512]{2,1,0:T(8,128)(2,1)}, u32[]{:S(2)}, u32[]{:S(2)}) %all-to-all-start.1) | async-done | bytes 4194336 | tf_op jit(solution)/shard_map/all_to_all | solution.py:34
  94.9 7.0 %fusion.7 = f32[32,128,512]{2,1,0:T(8,128)} fusion(bf16[32,128,512]{2,1,0:T(8,128)(2,1)} %all-to-all-done.1, bf16[32,6,128,128]{3,2,0,1:T(8,128)(2,1)} %bitcast_select_fusion), kind=kOutput, calls=%fused_computation.25 | convolution fusion | flops 536870912 | bytes 13631488 | tf_op jit(solution)/shard_map/pij,pjk->pik/dot_general | solution.py:37
  101.9 3.4 broadcast_in_dim.14
  105.2 18.6 %scatter_fusion = f32[24,128,512]{2,1,0:T(8,128)} fusion(f32[24,128,512]{2,1,0:T(8,128)} %broadcast_in_dim.14, s32[32]{0:T(128)S(1)} %get-tuple-element.10, f32[32,128,512]{2,1,0:T(8,128)} %fusion.7), kind=kCustom, calls=%fused_computation.1 | custom fusion | flops 2097152 | bytes 25165952 | tf_op jit(solution)/shard_map/scatter-add | solution.py:40
  123.8 7.0 %fusion.6 = f32[32,128,512]{2,1,0:T(8,128)} fusion(bf16[32,128,512]{2,1,0:T(8,128)(2,1)} %all-to-all-done.1, bf16[32,6,128,128]{3,2,0,1:T(8,128)(2,1)} %bitcast_select_fusion), kind=kOutput, calls=%fused_computation.23 | convolution fusion | flops 536870912 | bytes 13631488 | tf_op jit(solution)/shard_map/pij,pjk->pik/dot_general | solution.py:37
  130.8 18.6 %scatter_fusion.1 = f32[24,128,512]{2,1,0:T(8,128)} fusion(f32[24,128,512]{2,1,0:T(8,128)} %scatter_fusion, s32[32]{0:T(128)S(1)} %get-tuple-element.9, f32[32,128,512]{2,1,0:T(8,128)} %fusion.6), kind=kCustom, calls=%fused_computation.2 | custom fusion | flops 2097152 | bytes 25165952 | tf_op jit(solution)/shard_map/scatter-add | solution.py:40
  149.3 7.0 %fusion.5 = f32[32,128,512]{2,1,0:T(8,128)} fusion(bf16[32,128,512]{2,1,0:T(8,128)(2,1)} %all-to-all-done.1, bf16[32,6,128,128]{3,2,0,1:T(8,128)(2,1)} %bitcast_select_fusion), kind=kOutput, calls=%fused_computation.21 | convolution fusion | flops 536870912 | bytes 13631488 | tf_op jit(solution)/shard_map/pij,pjk->pik/dot_general | solution.py:37
  156.3 18.6 %scatter_fusion.2 = f32[24,128,512]{2,1,0:T(8,128)} fusion(f32[24,128,512]{2,1,0:T(8,128)} %scatter_fusion.1, s32[32]{0:T(128)S(1)} %get-tuple-element.8, f32[32,128,512]{2,1,0:T(8,128)} %fusion.5), kind=kCustom, calls=%fused_computation.3 | custom fusion | flops 2097152 | bytes 25165952 | tf_op jit(solution)/shard_map/scatter-add | solution.py:40
  175.0 7.0 %fusion.4 = f32[32,128,512]{2,1,0:T(8,128)} fusion(bf16[32,128,512]{2,1,0:T(8,128)(2,1)} %all-to-all-done.1, bf16[32,6,128,128]{3,2,0,1:T(8,128)(2,1)} %bitcast_select_fusion), kind=kOutput, calls=%fused_computation.19 | convolution fusion | flops 536870912 | bytes 13631488 | tf_op jit(solution)/shard_map/pij,pjk->pik/dot_general | solution.py:37
  181.9 18.5 %scatter_fusion.3 = f32[24,128,512]{2,1,0:T(8,128)} fusion(f32[24,128,512]{2,1,0:T(8,128)} %scatter_fusion.2, s32[32]{0:T(128)S(1)} %get-tuple-element.7, f32[32,128,512]{2,1,0:T(8,128)} %fusion.4), kind=kCustom, calls=%fused_computation.4 | custom fusion | flops 2097152 | bytes 25165952 | tf_op jit(solution)/shard_map/scatter-add | solution.py:40
  200.4 7.0 %fusion.3 = f32[32,128,512]{2,1,0:T(8,128)} fusion(bf16[32,128,512]{2,1,0:T(8,128)(2,1)} %all-to-all-done.1, bf16[32,6,128,128]{3,2,0,1:T(8,128)(2,1)} %bitcast_select_fusion), kind=kOutput, calls=%fused_computation.17 | convolution fusion | flops 536870912 | bytes 13631488 | tf_op jit(solution)/shard_map/pij,pjk->pik/dot_general | solution.py:37
  207.4 18.5 %scatter_fusion.4 = f32[24,128,512]{2,1,0:T(8,128)} fusion(f32[24,128,512]{2,1,0:T(8,128)} %scatter_fusion.3, s32[32]{0:T(128)S(1)} %get-tuple-element.6, f32[32,128,512]{2,1,0:T(8,128)} %fusion.3), kind=kCustom, calls=%fused_computation.5 | custom fusion | flops 2097152 | bytes 25165952 | tf_op jit(solution)/shard_map/scatter-add | solution.py:40
  225.9 7.0 %fusion.2 = f32[32,128,512]{2,1,0:T(8,128)} fusion(bf16[32,128,512]{2,1,0:T(8,128)(2,1)} %all-to-all-done.1, bf16[32,6,128,128]{3,2,0,1:T(8,128)(2,1)} %bitcast_select_fusion), kind=kOutput, calls=%fused_computation.15 | convolution fusion | flops 536870912 | bytes 13631488 | tf_op jit(solution)/shard_map/pij,pjk->pik/dot_general | solution.py:37
  232.9 18.4 %scatter_fusion.5 = f32[24,128,512]{2,1,0:T(8,128)} fusion(f32[24,128,512]{2,1,0:T(8,128)} %scatter_fusion.4, s32[32]{0:T(128)S(1)} %get-tuple-element.5, f32[32,128,512]{2,1,0:T(8,128)} %fusion.2), kind=kCustom, calls=%fused_computation.6 | custom fusion | flops 2097152 | bytes 25165952 | tf_op jit(solution)/shard_map/scatter-add | solution.py:40
  251.3 3.7 broadcast_multiply_fusion
  255.0 1.3 fusion
  256.3 1.5 subtract_convert_fusion
  257.8 1.8 fusion.15
  259.6 2.9 fusion.1
  262.5 0.0 all-reduce.3.cloned.1.call-update
  262.5 258.2 %all-reduce.3.cloned.1.call-done = f32[512,512]{0,1:T(8,128)} async-done(((f32[512,512]{0,1:T(8,128)}), f32[512,512]{0,1:T(8,128)}) %all-reduce.3.cloned.1.call-update) | async-done | bytes 1048592
  520.7 1.1 constant_dynamic-slice_fusion
  521.8 0.1 copy.16
  521.9 0.6 broadcast_multiply_fusion.1
  (10 shorter events, 0.0 us)
Async XLA Ops:
  28.8 5.0 copy-start.1
  28.8 5.1 copy-start.2
  28.8 66.1 %all-to-all-start.1 = ((bf16[32,128,512]{2,1,0:T(8,128)(2,1)}), bf16[32,128,512]{2,1,0:T(8,128)(2,1)}, u32[]{:S(2)}, u32[]{:S(2)}) async-start(bf16[32,128,512]{2,1,0:T(8,128)(2,1)} %gather_fusion), calls=%async_computation.1 | async-start | bytes 8388608 | tf_op jit(solution)/shard_map/all_to_all | solution.py:34
  33.7 486.9 %all-reduce.3.cloned.1.call-start = ((), (), s32[]{:S(2)}) async-start(), calls=%async_computation.2 | async-start | bytes 2097152
  251.3 3.7 copy-start
Sparse Core Ops, SparseCore 0:
  262.6 258.0 all-reduce.2
where the time goes:
time: 531 us; the launch traced here: 529 us
  waiting for transfers between devices  313 us (59%)
  other arithmetic  126 us (24%)
  matrix products  46.5 us (9%)
  blocking collectives  16.1 us (3%)
  between operations  13.5 us (3%)
  local copies, waits for them, and re-layouts  9.98 us (2%)
    unnamed x2, waiting for transfers between devices  258 us
    scatter-add x6, other arithmetic, body(): running = running.at[target_rows[:, which]].add(product)  111 us
    all_to_all x1, waiting for transfers between devices, body(): lax.all_to_all(outgoing, 'state', split_axis=0, concat_axis=0, tiled=True)  54.4 us
    dot_general x6, matrix products, body(): jnp.einsum('pij,pjk->pik', tile_set[:, which], received, preferred_elemen...  41.8 us
    all_to_all x1, blocking collectives, body(): lax.all_to_all(wanted_cols, 'state', split_axis=0, concat_axis=0, tiled=T...  16.1 us
  transfers between devices with their start and end apart: 2, of which 2 were waited for; matrix products, arithmetic and copies ran while one was open for 1% of the time, Pallas kernels for 0%

commit v1 on v0

v1 whole, which is shorter than its diff:
```python
import functools
import math

import jax
import jax.numpy as jnp
from jax import lax
from jax.experimental import pallas as pl
from jax.experimental.pallas import tpu as pltpu
from jax.sharding import PartitionSpec as P

discount = 0.95


def tile_kernel(
    start_ref, rows_ref, counts_ref, tiles_ref, phi_ref, high_ref, low_ref, gram_ref, turned
):
    step = pl.program_id(0)
    block_count = phi_ref.shape[0]
    use_count = tiles_ref.shape[1]

    @pl.when(step == 0)
    def _():
        def turn(b, carry):
            turned[b] = phi_ref[b].T
            return carry

        lax.fori_loop(0, block_count, turn, 0)
        gram_ref[...] = jnp.zeros_like(gram_ref)

        def gram(b, carry):
            gram_ref[...] += jnp.dot(turned[b], phi_ref[b], preferred_element_type=jnp.float32)
            return carry

        lax.fori_loop(start_ref[0], start_ref[1], gram, 0)

    count = counts_ref[step]
    left = jnp.concatenate(
        [turned[rows_ref[step * use_count + u]] for u in range(use_count)], axis=1
    )
    right = jnp.concatenate(
        [
            jnp.where(u < count, tiles_ref[0, u], jnp.zeros((), tiles_ref.dtype))
            for u in range(use_count)
        ],
        axis=0,
    )
    product = jnp.dot(left, right, preferred_element_type=jnp.float32) * (-discount)
    high = product.astype(jnp.bfloat16)
    high_ref[...] = high
    low_ref[...] = (product - high.astype(jnp.float32)).astype(jnp.bfloat16)


def apply_tiles(span, rows, counts, tiles, blocks):
    peers, use_count, tile_size, _ = tiles.shape
    block_count, _, features = blocks.shape
    wide = jax.ShapeDtypeStruct((features, peers * tile_size), jnp.bfloat16)
    return pl.pallas_call(
        tile_kernel,
        out_shape=(wide, wide, jax.ShapeDtypeStruct((features, features), jnp.float32)),
        grid_spec=pltpu.PrefetchScalarGridSpec(
            num_scalar_prefetch=3,
            grid=(peers,),
            in_specs=[
                pl.BlockSpec((1, use_count, tile_size, tile_size), lambda p, *_: (p, 0, 0, 0)),
                pl.BlockSpec((block_count, tile_size, features), lambda p, *_: (0, 0, 0)),
            ],
            out_specs=[
                pl.BlockSpec((features, tile_size), lambda p, *_: (0, p)),
                pl.BlockSpec((features, tile_size), lambda p, *_: (0, p)),
                pl.BlockSpec((features, features), lambda p, *_: (0, 0)),
            ],
            scratch_shapes=[pltpu.VMEM((block_count, features, tile_size), jnp.bfloat16)],
        ),
        compiler_params=pltpu.CompilerParams(vmem_limit_bytes=24 << 20),
        cost_estimate=pl.CostEstimate(
            flops=2 * peers * use_count * tile_size * tile_size * features,
            bytes_accessed=2 * tiles.size + 2 * blocks.size + 4 * wide.size,
            transcendentals=0,
        ),
        name="apply_tiles",
    )(span, rows, counts, tiles, blocks)


def join_kernel(high_ref, low_ref, source_ref, gram_ref, out_ref):
    @pl.when(pl.program_id(0) == 0)
    def _():
        out_ref[...] = gram_ref[...]

    source = source_ref[...]
    out_ref[...] += jnp.dot(high_ref[...], source, preferred_element_type=jnp.float32) + jnp.dot(
        low_ref[...], source, preferred_element_type=jnp.float32
    )


def join(high, low, source, gram, steps=8):
    features, depth = high.shape
    chunk = depth // steps
    return pl.pallas_call(
        join_kernel,
        out_shape=jax.ShapeDtypeStruct((features, features), jnp.float32),
        grid=(steps,),
        in_specs=[
            pl.BlockSpec((features, chunk), lambda k: (0, k)),
            pl.BlockSpec((features, chunk), lambda k: (0, k)),
            pl.BlockSpec((chunk, features), lambda k: (k, 0)),
            pl.BlockSpec((features, features), lambda k: (0, 0)),
        ],
        out_specs=pl.BlockSpec((features, features), lambda k: (0, 0)),
        compiler_params=pltpu.CompilerParams(vmem_limit_bytes=16 << 20),
        cost_estimate=pl.CostEstimate(
            flops=4 * features * depth * features,
            bytes_accessed=6 * features * depth,
            transcendentals=0,
        ),
        name="join",
    )(high, low, source, gram)


def body(basis_rows, tile_blocks, tile_cols, tile_rows, tile_counts):
    shards = lax.axis_size("state")
    groups = lax.axis_size("group")
    local_rows, features = basis_rows.shape
    tile_size = tile_blocks.shape[-1]
    block_count = local_rows // tile_size
    blocks = basis_rows.reshape(block_count, tile_size, features)
    exchange = functools.partial(lax.all_to_all, split_axis=0, concat_axis=0, tiled=True)

    asked_cols = exchange(tile_cols[0, 0], "state")
    received = exchange(blocks[asked_cols], "state")

    member = lax.axis_index("group")
    span = jnp.stack([member * block_count // groups, (member + 1) * block_count // groups])
    high, low, gram = apply_tiles(
        span.astype(jnp.int32),
        tile_rows[0, 0].reshape(-1),
        tile_counts[0, 0],
        tile_blocks[0, 0],
        blocks,
    )
    partial = join(high, low, received.reshape(-1, features), gram)

    first = exchange(partial.reshape(shards, features // shards, features), "state").sum(0)
    final = exchange(first.reshape(groups, -1, features), "group").sum(0)
    return final * (1.0 / math.sqrt(local_rows * shards))


def solution(mesh):
    in_specs = (
        P("state", None),
        P("state", "group", None, None, None, None),
        P("state", "group", None),
        P("state", "group", None, None),
        P("state", "group", None),
    )
    out_specs = P(("state", "group"), None)
    return jax.shard_map(body, mesh=mesh, in_specs=in_specs, out_specs=out_specs, check_vma=False)
```

time: 531 us -> 140 us (0.26)
  waiting for transfers between devices: 313 us -> 35 us
  other arithmetic: 126 us -> 1.44 us
  matrix products: 46.5 us -> 0 us
  blocking collectives: 16.1 us -> 52.4 us
  Pallas kernels: 0 us -> 26.5 us
  between operations: 13.5 us -> 0.1 us
  local copies, waits for them, and re-layouts: 9.98 us -> 18.8 us
    unnamed x2 -> x0, waiting for transfers between devices: 258 us -> none
    scatter-add x6 -> x0, other arithmetic: 111 us -> none  [body(): running = running.at[target_rows[:, which]].add(product)]
    dot_general x8 -> x0, matrix products: 46.5 us -> none  [the longest x6 41.8 us: body(): jnp.einsum('pij,pjk->pik', tile_set[:, which], received, preferred_elemen...]
    all_to_all x1 -> x3, blocking collectives: 16.1 us -> 52.4 us  [the longest x1 18.9 us: body(): exchange(partial.reshape(shards, features // shards, features), 'state')]
    pallas_call x0 -> x2, Pallas kernels: none -> 26.5 us  [the longest x1 18.2 us: apply_tiles(): pl.pallas_call(tile_kernel, out_shape=(wide, wide, jax.ShapeDtypeStruct((...]
    all_to_all x1, waiting for transfers between devices: 54.4 us -> 35 us  [body(): received = exchange(blocks[asked_cols], 'state')]
    unnamed x8 -> x21, local copies, waits for them, and re-layouts: 1.09 us -> 13.3 us
    select_n x3 -> x1, other arithmetic: 6.64 us -> 0.01 us  [body(): received = exchange(blocks[asked_cols], 'state')]
  transfers between devices with their start and end apart: 2 -> 1, of which waited for: 2 -> 1; matrix products, arithmetic and copies ran while one was open for 1% -> 0% of each run, Pallas kernels for 0% -> 13%
where the time goes in v1:
time: 140 us; the launch traced here: 139 us
  blocking collectives  52.4 us (37%)
  waiting for transfers between devices  35 us (25%)
  Pallas kernels  26.5 us (19%)
  local copies, waits for them, and re-layouts  18.8 us (13%)
  starting transfers between devices  5.13 us (4%)
  other arithmetic  1.44 us (1%)
    all_to_all x1, waiting for transfers between devices, body(): received = exchange(blocks[asked_cols], 'state')  35 us
    all_to_all x1, blocking collectives, body(): exchange(partial.reshape(shards, features // shards, features), 'state')  18.9 us
    pallas_call x1, Pallas kernels, apply_tiles(): pl.pallas_call(tile_kernel, out_shape=(wide, wide, jax.ShapeDtypeStruct((...  18.2 us
    all_to_all x1, blocking collectives, body(): final = exchange(first.reshape(groups, -1, features), 'group').sum(0)  17.4 us
    all_to_all x1, blocking collectives, body(): asked_cols = exchange(tile_cols[0, 0], 'state')  16.1 us
    unnamed x21, local copies, waits for them, and re-layouts  13.3 us
    pallas_call x1, Pallas kernels, join(): pl.pallas_call(join_kernel, out_shape=jax.ShapeDtypeStruct((features, fea...  8.35 us
    all_to_all x1, starting transfers between devices, body(): received = exchange(blocks[asked_cols], 'state')  5.13 us
  transfers between devices with their start and end apart: 1, of which 1 were waited for; matrix products, arithmetic and copies ran while one was open for 0% of the time, Pallas kernels for 13%

profile of v1, /device:TPU:1, one launch (start us, length us, event | category | flops | bytes accessed | tf_op | source)
XLA Modules:
  0.0 139.5 jit_solution(10390365579881782075)
XLA Ops:
  0.0 0.7 copy.14
  0.7 16.1 %all_to_all.27 = s32[32,1,1]{2,1,0:T(1,128)S(1)} all-to-all(s32[32,1,1]{2,1,0:T(1,128)S(1)} %copy.14), channel_id=1, replica_groups=mesh['state'=32,'group'=8] {'state'}, dimensions={0} | all-to-all | bytes 256 | tf_op jit(solution)/shard_map/all_to_all | solution.py:128
  16.9 0.7 reduce
  17.5 4.7 %gather_fusion = bf16[32,128,512]{2,1,0:T(8,128)(2,1)} fusion(bf16[24,128,512]{2,1,0:T(8,128)(2,1)} %bitcast.14, s32[1024]{0:T(1024)S(1)} %pad_clamp_fusion), kind=kCustom, calls=%fused_computation | custom fusion | bytes 8388736 | tf_op jit(solution)/shard_map/gather | solution.py:129
  22.2 0.0 copy-start.9
  22.2 0.0 copy-start
  22.2 0.0 copy-start.2
  22.2 5.1 %all-to-all-start.1 = ((bf16[32,128,512]{2,1,0:T(8,128)(2,1)}), bf16[32,128,512]{2,1,0:T(8,128)(2,1)}, u32[]{:S(2)}, u32[]{:S(2)}) async-start(bf16[32,128,512]{2,1,0:T(8,128)(2,1)} %gather_fusion), calls=%async_computation.1 | async-start | bytes 8388608 | tf_op jit(solution)/shard_map/all_to_all | solution.py:129
  27.4 0.0 copy-done.9
  27.4 0.1 copy.13
  27.5 0.1 reshape_squeeze.3.rows_ref
  27.6 0.1 pad_add_fusion.start_ref
  27.7 0.0 copy-done
  27.7 0.0 copy-done.2
  27.7 0.0 copy-start.1
  27.7 2.8 %copy-done.1 = bf16[1,1,32,6,128,128]{5,4,3,2,1,0:T(8,128)(2,1)S(1)} copy-done((bf16[1,1,32,6,128,128]{5,4,3,2,1,0:T(8,128)(2,1)S(1)}, bf16[1,1,32,6,128,128]{5,4,3,2,1,0:T(8,128)(2,1)}, u32[]{:S(2)}) %copy-start.1) | copy-done | bytes 6291480
  30.4 18.2 %apply_tiles.1 = (bf16[512,4096]{1,0:T(8,128)(2,1)S(1)}, bf16[512,4096]{1,0:T(8,128)(2,1)S(1)}, f32[512,512]{1,0:T(8,128)S(1)}) custom-call(s32[2]{0:T(128)S(1)} %pad_add_fusion.start_ref, s32[192]{0:T(256)S(1)} %reshape_squeeze.3.rows_ref, s32[32]{0:T(128)S(1)} %bitcast.18, bf16[32,6,128,128]{3,2,1,0:T(8,128)(2,1)S(1)} %bitcast.17, ...), custom_call_target="tpu_custom_call" | custom-call | flops 3221225472 | bytes 17825792 | tf_op jit(solution)/shard_map/apply_tiles/pallas_call | solution.py:57
  48.6 0.0 copy-start.3
  48.6 1.9 %copy-done.3 = bf16[512,4096]{1,0:T(8,128)(2,1)} copy-done((bf16[512,4096]{1,0:T(8,128)(2,1)}, bf16[512,4096]{1,0:T(8,128)(2,1)S(1)}, u32[]{:S(2)}) %copy-start.3) | copy-done | bytes 4194328
  50.6 0.0 copy-start.5
  50.6 1.9 %copy-done.5 = bf16[512,4096]{1,0:T(8,128)(2,1)} copy-done((bf16[512,4096]{1,0:T(8,128)(2,1)}, bf16[512,4096]{1,0:T(8,128)(2,1)S(1)}, u32[]{:S(2)}) %copy-start.5) | copy-done | bytes 4194328
  52.5 0.0 copy-start.7
  52.5 1.0 copy-done.7
  53.5 35.0 %all-to-all-done.1 = bf16[32,128,512]{2,1,0:T(8,128)(2,1)} async-done(((bf16[32,128,512]{2,1,0:T(8,128)(2,1)}), bf16[32,128,512]{2,1,0:T(8,128)(2,1)}, u32[]{:S(2)}, u32[]{:S(2)}) %all-to-all-start.1) | async-done | bytes 4194336 | tf_op jit(solution)/shard_map/all_to_all | solution.py:129
  88.5 2.2 %copy-done.4 = bf16[512,4096]{1,0:T(8,128)(2,1)S(1)} copy-done((bf16[512,4096]{1,0:T(8,128)(2,1)S(1)}, bf16[512,4096]{1,0:T(8,128)(2,1)}, u32[]{:S(2)}) %copy-start.4) | copy-done | bytes 4194328
  90.7 2.2 %copy-done.6 = bf16[512,4096]{1,0:T(8,128)(2,1)S(1)} copy-done((bf16[512,4096]{1,0:T(8,128)(2,1)S(1)}, bf16[512,4096]{1,0:T(8,128)(2,1)}, u32[]{:S(2)}) %copy-start.6) | copy-done | bytes 4194328
  92.9 1.2 copy-done.8
  94.1 8.3 %join.1 = f32[512,512]{1,0:T(8,128)S(1)} custom-call(bf16[512,4096]{1,0:T(8,128)(2,1)S(1)} %copy-done.4, bf16[512,4096]{1,0:T(8,128)(2,1)S(1)} %copy-done.6, bf16[4096,512]{1,0:T(8,128)(2,1)} %bitcast.7.source_ref, f32[512,512]{1,0:T(8,128)S(1)} %copy-done.8), custom_call_target="tpu_custom_call" | custom-call | flops 4294967296 | bytes 12582912 | tf_op jit(solution)/shard_map/join/pallas_call | solution.py:98
  102.4 18.9 %all_to_all.28 = f32[32,16,512]{2,1,0:T(8,128)S(1)} all-to-all(f32[32,16,512]{2,1,0:T(8,128)S(1)} %bitcast.16), channel_id=1, replica_groups=mesh['state'=32,'group'=8] {'state'}, dimensions={0} | all-to-all | bytes 2097152 | tf_op jit(solution)/shard_map/all_to_all | solution.py:142
  121.3 0.1 reduce_sum.18
  121.4 17.4 %all_to_all.29 = f32[8,2,512]{2,1,0:T(2,128)S(1)} all-to-all(f32[8,2,512]{2,1,0:T(2,128)S(1)} %reshape.46), channel_id=1, replica_groups=mesh['state'=32,'group'=8] {'group'}, dimensions={0} | all-to-all | bytes 65536 | tf_op jit(solution)/shard_map/all_to_all | solution.py:143
  138.9 0.6 broadcast_multiply_fusion
  (7 shorter events, 0.1 us)
Async XLA Ops:
  22.2 5.2 %copy-start.9 = (s32[1,1,32,6]{2,1,3,0:T(1,128)S(1)}, s32[1,1,32,6]{2,1,3,0:T(1,128)}, u32[]{:S(2)}) copy-start(s32[1,1,32,6]{2,1,3,0:T(1,128)} %param.8) | copy-start | bytes 2308
  22.2 5.5 %copy-start = (bf16[3072,512]{1,0:T(8,128)(2,1)S(1)}, bf16[3072,512]{1,0:T(8,128)(2,1)}, u32[]{:S(2)}) copy-start(bf16[3072,512]{1,0:T(8,128)(2,1)} %param.5) | copy-start | bytes 9437188
  22.2 5.5 %copy-start.2 = (s32[1,1,32]{2,1,0:T(1,128)S(1)}, s32[1,1,32]{2,1,0:T(1,128)}, u32[]{:S(2)}) copy-start(s32[1,1,32]{2,1,0:T(1,128)} %param.9) | copy-start | bytes 388
  22.2 66.3 %all-to-all-start.1 = ((bf16[32,128,512]{2,1,0:T(8,128)(2,1)}), bf16[32,128,512]{2,1,0:T(8,128)(2,1)}, u32[]{:S(2)}, u32[]{:S(2)}) async-start(bf16[32,128,512]{2,1,0:T(8,128)(2,1)} %gather_fusion), calls=%async_computation.1 | async-start | bytes 8388608 | tf_op jit(solution)/shard_map/all_to_all | solution.py:129
  27.7 2.8 %copy-start.1 = (bf16[1,1,32,6,128,128]{5,4,3,2,1,0:T(8,128)(2,1)S(1)}, bf16[1,1,32,6,128,128]{5,4,3,2,1,0:T(8,128)(2,1)}, u32[]{:S(2)}) copy-start(bf16[1,1,32,6,128,128]{5,4,3,2,1,0:T(8,128)(2,1)} %param.6) | copy-start | bytes 18874372
  48.6 1.9 %copy-start.3 = (bf16[512,4096]{1,0:T(8,128)(2,1)}, bf16[512,4096]{1,0:T(8,128)(2,1)S(1)}, u32[]{:S(2)}) copy-start(bf16[512,4096]{1,0:T(8,128)(2,1)S(1)} %get-tuple-element.8.high_ref) | copy-start | bytes 12582916
  50.6 1.9 %copy-start.5 = (bf16[512,4096]{1,0:T(8,128)(2,1)}, bf16[512,4096]{1,0:T(8,128)(2,1)S(1)}, u32[]{:S(2)}) copy-start(bf16[512,4096]{1,0:T(8,128)(2,1)S(1)} %get-tuple-element.9.low_ref) | copy-start | bytes 12582916
  52.5 1.0 copy-start.7
  88.5 2.2 %copy-start.4 = (bf16[512,4096]{1,0:T(8,128)(2,1)S(1)}, bf16[512,4096]{1,0:T(8,128)(2,1)}, u32[]{:S(2)}) copy-start(bf16[512,4096]{1,0:T(8,128)(2,1)} %copy-done.3) | copy-start | bytes 12582916
  90.7 2.2 %copy-start.6 = (bf16[512,4096]{1,0:T(8,128)(2,1)S(1)}, bf16[512,4096]{1,0:T(8,128)(2,1)}, u32[]{:S(2)}) copy-start(bf16[512,4096]{1,0:T(8,128)(2,1)} %copy-done.5) | copy-start | bytes 12582916
  92.9 1.2 copy-start.8

commit v2 on v0

v2 whole, which is shorter than its diff:
```python
import functools
import math

import jax
import jax.numpy as jnp
from jax import lax
from jax.experimental import pallas as pl
from jax.experimental.pallas import tpu as pltpu
from jax.sharding import PartitionSpec as P


discount = 0.95
extra_rows = 16
first_features = 128
peers_per_step = 4


def dot(left, right):
    return jnp.dot(left, right, preferred_element_type=jnp.float32)


def apply_kernel(
    start, with_cols, rows_ref, counts_ref, cols_ref, tiles_ref, phi_ref, out_ref, turned
):
    step = pl.program_id(0)
    block_count, features, _ = turned.shape
    peers, use_count = tiles_ref.shape[:2]

    @pl.when(step == 0)
    def _():
        def turn(b, carry):
            turned[b] = phi_ref[b, :, start : start + features].T
            return carry

        lax.fori_loop(0, block_count, turn, 0)

    for local in range(peers):
        peer = step * peers + local
        count = counts_ref[peer]
        left = jnp.concatenate(
            [turned[rows_ref[peer * use_count + u]] for u in range(use_count)], axis=1
        )
        right = jnp.concatenate(
            [
                jnp.where(u < count, tiles_ref[local, u], jnp.zeros((), tiles_ref.dtype))
                for u in range(use_count)
            ],
            axis=0,
        )
        product = dot(left, right) * (-discount)
        out_ref[local, :features] = product.astype(out_ref.dtype)
        if with_cols:
            column = jnp.full((extra_rows, out_ref.shape[2]), cols_ref[peer], jnp.int32)
            out_ref[local, features:] = column.astype(jnp.float32).astype(out_ref.dtype)


def apply_tiles(rows, counts, cols, tiles, blocks, start, size, with_cols):
    peers, use_count, tile_size, _ = tiles.shape
    block_count = blocks.shape[0]
    height = size + (extra_rows if with_cols else 0)
    per_step = peers_per_step
    return pl.pallas_call(
        functools.partial(apply_kernel, start, with_cols),
        out_shape=jax.ShapeDtypeStruct((peers, height, tile_size), jnp.bfloat16),
        grid_spec=pltpu.PrefetchScalarGridSpec(
            num_scalar_prefetch=3,
            grid=(peers // per_step,),
            in_specs=[
                pl.BlockSpec(
                    (per_step, use_count, tile_size, tile_size), lambda p, *_: (p, 0, 0, 0)
                ),
                pl.BlockSpec((block_count, tile_size, blocks.shape[2]), lambda p, *_: (0, 0, 0)),
            ],
            out_specs=pl.BlockSpec((per_step, height, tile_size), lambda p, *_: (p, 0, 0)),
            scratch_shapes=[pltpu.VMEM((block_count, size, tile_size), jnp.bfloat16)],
        ),
        cost_estimate=pl.CostEstimate(
            flops=2 * peers * use_count * tile_size * tile_size * size,
            bytes_accessed=2 * (tiles.size + blocks.size + peers * height * tile_size),
            transcendentals=0,
        ),
        name="apply_tiles",
    )(rows, counts, cols, tiles, blocks)


def join_kernel(gram_blocks, start, spot_ref, cols_ref, phi_ref, sent_ref, keep_ref, give_ref, total):
    step = pl.program_id(0)
    height, features = total.shape
    peers = sent_ref.shape[0]

    @pl.when(step == 0)
    def _():
        own = [phi_ref[spot_ref[0] * gram_blocks + b] for b in range(gram_blocks)]
        tall = jnp.concatenate(own, axis=0)
        part = tall[:, start : start + height]
        total[...] = lax.dot_general(
            part, tall, (((0,), (0,)), ((), ())), preferred_element_type=jnp.float32
        )

    left = jnp.concatenate([sent_ref[s, :height] for s in range(peers)], axis=1)
    right = jnp.concatenate([phi_ref[cols_ref[step * peers + s]] for s in range(peers)], axis=0)
    total[...] += dot(left, right)

    @pl.when(step == pl.num_programs(0) - 1)
    def _():
        rows = total[...].reshape(height // 16, 2, 8, features)
        even, odd = rows[:, 0], rows[:, 1]
        place = lax.broadcasted_iota(jnp.int32, even.shape, 1)
        lower = lax.rem(place, 4) < 2
        zero = jnp.where(lower, even, jnp.roll(odd, 2, axis=1))
        one = jnp.where(lower, jnp.roll(even, -2, axis=1), odd)
        own_one = spot_ref[1] == 1
        keep_ref[...] = jnp.where(own_one, one, zero)
        give_ref[...] = jnp.where(own_one, zero, one)


def join(spot, cols, blocks, sent, gram_blocks, start, size):
    peers, height, tile_size = sent.shape
    block_count, _, features = blocks.shape
    per_step = 8
    half = jax.ShapeDtypeStruct((size // 16, 8, features), jnp.float32)
    return pl.pallas_call(
        functools.partial(join_kernel, gram_blocks, start),
        out_shape=(half, half),
        grid_spec=pltpu.PrefetchScalarGridSpec(
            num_scalar_prefetch=2,
            grid=(peers // per_step,),
            in_specs=[
                pl.BlockSpec((block_count, tile_size, features), lambda p, *_: (0, 0, 0)),
                pl.BlockSpec((per_step, height, tile_size), lambda p, *_: (p, 0, 0)),
            ],
            out_specs=[
                pl.BlockSpec((size // 16, 8, features), lambda p, *_: (0, 0, 0)),
                pl.BlockSpec((size // 16, 8, features), lambda p, *_: (0, 0, 0)),
            ],
            scratch_shapes=[pltpu.VMEM((size, features), jnp.float32)],
        ),
        compiler_params=pltpu.CompilerParams(vmem_limit_bytes=24 << 20),
        cost_estimate=pl.CostEstimate(
            flops=2 * peers * tile_size * size * features,
            bytes_accessed=2 * (blocks.size + sent.size) + 8 * size * features,
            transcendentals=0,
        ),
        name="join",
    )(spot, cols, blocks, sent)


def body(basis_rows, tile_blocks, tile_cols, tile_rows, tile_counts):
    shards = lax.axis_size("state")
    groups = lax.axis_size("group")
    local_rows, features = basis_rows.shape
    tile_size = tile_blocks.shape[-1]
    block_count = local_rows // tile_size
    blocks = basis_rows.reshape(block_count, tile_size, features)
    exchange = functools.partial(
        lax.all_to_all, axis_name="state", split_axis=0, concat_axis=0, tiled=True
    )
    swap = [(g, g ^ 1) for g in range(groups)]
    member = lax.axis_index("group")
    spot = jnp.stack([member, member & 1]).astype(jnp.int32)

    rows = tile_rows[0, 0].reshape(-1)
    counts = tile_counts[0, 0]
    cols = tile_cols[0, 0]
    tiles = tile_blocks[0, 0]
    rest = features - first_features
    gram_blocks = block_count // groups

    sent = apply_tiles(rows, counts, cols, tiles, blocks, 0, first_features, True)
    got_one = exchange(sent)
    sent = apply_tiles(rows, counts, cols, tiles, blocks, first_features, rest, False)
    got_two = exchange(sent)
    wanted = got_one[:, first_features, 0].astype(jnp.int32)
    keep_one, give_one = join(spot, wanted, blocks, got_one, gram_blocks, 0, first_features)
    keep_two, give_two = join(spot, wanted, blocks, got_two, gram_blocks, first_features, rest)
    half = jnp.concatenate(
        [
            keep_one + lax.ppermute(give_one, "group", swap),
            keep_two + lax.ppermute(give_two, "group", swap),
        ],
        axis=0,
    )
    owned = exchange(half).sum(0)

    quads = groups // 2
    quad = member >> 1
    final = lax.dynamic_slice_in_dim(owned, 2 * place_of(quad), 2, 0)
    for shift in range(1, quads):
        target = lax.rem(quad + shift, quads)
        piece = lax.dynamic_slice_in_dim(owned, 2 * place_of(target), 2, 0)
        ring = [(g, (g + 2 * shift) % groups) for g in range(groups)]
        final = final + lax.ppermute(piece, "group", ring)
    return final * (1.0 / math.sqrt(local_rows * shards))


def place_of(quad):
    return (quad & 1) * 2 + (quad >> 1)


def solution(mesh):
    in_specs = (
        P("state", None),
        P("state", "group", None, None, None, None),
        P("state", "group", None),
        P("state", "group", None, None),
        P("state", "group", None),
    )
    out_specs = P(("state", "group"), None)
    return jax.shard_map(body, mesh=mesh, in_specs=in_specs, out_specs=out_specs, check_vma=False)
```

time: 531 us -> 133 us (0.25)
  waiting for transfers between devices: 313 us -> 62.4 us
  other arithmetic: 126 us -> 3.13 us
  matrix products: 46.5 us -> 0 us
  Pallas kernels: 0 us -> 33.6 us
  starting transfers between devices: 5.02 us -> 30.6 us
  blocking collectives: 16.1 us -> 0 us
  between operations: 13.5 us -> 0.11 us
  local copies, waits for them, and re-layouts: 9.98 us -> 1.45 us
    unnamed x2 -> x0, waiting for transfers between devices: 258 us -> none
    scatter-add x6 -> x0, other arithmetic: 111 us -> none  [body(): running = running.at[target_rows[:, which]].add(product)]
    dot_general x8 -> x0, matrix products: 46.5 us -> none  [the longest x6 41.8 us: body(): jnp.einsum('pij,pjk->pik', tile_set[:, which], received, preferred_elemen...]
    pallas_call x0 -> x4, Pallas kernels: none -> 33.6 us  [the longest x2 24.7 us: apply_tiles(): pl.pallas_call(functools.partial(apply_kernel, start, with_cols), out_sha...]
    all_to_all x1 -> x0, blocking collectives: 16.1 us -> none  [body(): lax.all_to_all(wanted_cols, 'state', split_axis=0, concat_axis=0, tiled=T...]
    all_to_all x1 -> x3, starting transfers between devices: 4.98 us -> 18.1 us  [the longest x1 9.32 us: body(): got_one = exchange(sent)]
    ppermute x0 -> x5, starting transfers between devices: none -> 12.6 us  [the longest x3 9.67 us: body(): final = final + lax.ppermute(piece, 'group', ring)]
    select_n x3 -> x0, other arithmetic: 6.64 us -> none  [the longest x1 6.62 us: body(): jnp.where(live_mask[:, :, None, None], tile_blocks[0, 0], jnp.zeros((), j...]
  transfers between devices with their start and end apart: 2 -> 8, of which waited for: 2 -> 5; matrix products, arithmetic and copies ran while one was open for 1% -> 1% of each run, Pallas kernels for 0% -> 13%
where the time goes in v2:
time: 133 us; the launch traced here: 131 us
  waiting for transfers between devices  62.4 us (47%)
  Pallas kernels  33.6 us (25%)
  starting transfers between devices  30.6 us (23%)
  other arithmetic  3.13 us (2%)
  local copies, waits for them, and re-layouts  1.45 us (1%)
    all_to_all x1, waiting for transfers between devices, body(): got_two = exchange(sent)  43.1 us
    pallas_call x2, Pallas kernels, apply_tiles(): pl.pallas_call(functools.partial(apply_kernel, start, with_cols), out_sha...  24.7 us
    all_to_all x1, waiting for transfers between devices, body(): owned = exchange(half).sum(0)  11.6 us
    ppermute x3, starting transfers between devices, body(): final = final + lax.ppermute(piece, 'group', ring)  9.67 us
    all_to_all x1, starting transfers between devices, body(): got_one = exchange(sent)  9.32 us
    pallas_call x2, Pallas kernels, join(): pl.pallas_call(functools.partial(join_kernel, gram_blocks, start), out_sh...  8.87 us
    all_to_all x1, starting transfers between devices, body(): got_two = exchange(sent)  4.82 us
    all_to_all x1, waiting for transfers between devices, body(): got_one = exchange(sent)  4.46 us
  transfers between devices with their start and end apart: 8, of which 5 were waited for; matrix products, arithmetic and copies ran while one was open for 1% of the time, Pallas kernels for 13%

profile of v2, /device:TPU:1, one launch (start us, length us, event | category | flops | bytes accessed | tf_op | source)
XLA Modules:
  0.0 131.4 jit_solution(2006371325427394757)
XLA Ops:
  0.0 0.8 copy.6
  0.8 0.7 reshape_squeeze.3.rows_ref
  1.4 11.0 %apply_tiles.2 = bf16[32,144,128]{2,1,0:T(8,128)(2,1)} custom-call(s32[192]{0:T(256)} %reshape_squeeze.3.rows_ref, s32[32]{0:T(128)} %bitcast.14, s32[32]{0:T(128)} %bitcast.16, bf16[32,6,128,128]{3,2,1,0:T(8,128)(2,1)} %bitcast.12, bf16[24,128,512]{2,1,0:T(8,128)(2,1)} %bitcast.8), custom_call_target="tpu_custom_call" | custom-call | flops 805306368 | bytes 10616832 | tf_op jit(solution)/shard_map/apply_tiles/pallas_call | solution.py:62
  12.5 9.3 %all-to-all-start = ((bf16[32,144,128]{2,1,0:T(8,128)(2,1)}), bf16[32,144,128]{2,1,0:T(8,128)(2,1)}, u32[]{:S(2)}, u32[]{:S(2)}) async-start(bf16[32,144,128]{2,1,0:T(8,128)(2,1)} %apply_tiles.2), calls=%async_computation | async-start | bytes 2359296 | tf_op jit(solution)/shard_map/all_to_all | solution.py:170
  21.8 13.7 %apply_tiles.3 = bf16[32,384,128]{2,1,0:T(8,128)(2,1)} custom-call(s32[192]{0:T(256)} %reshape_squeeze.3.rows_ref, s32[32]{0:T(128)} %bitcast.15, s32[32]{0:T(128)} %bitcast.17, bf16[32,6,128,128]{3,2,1,0:T(8,128)(2,1)} %bitcast.13, bf16[24,128,512]{2,1,0:T(8,128)(2,1)} %bitcast.9), custom_call_target="tpu_custom_call" | custom-call | flops 2415919104 | bytes 12582912 | tf_op jit(solution)/shard_map/apply_tiles/pallas_call | solution.py:62
  35.5 0.0 copy-start
  35.5 4.5 %all-to-all-done.sent_ref = bf16[32,144,128]{2,1,0:T(8,128)(2,1)} async-done(((bf16[32,144,128]{2,1,0:T(8,128)(2,1)}), bf16[32,144,128]{2,1,0:T(8,128)(2,1)}, u32[]{:S(2)}, u32[]{:S(2)}) %all-to-all-start) | async-done | bytes 1179680 | tf_op jit(solution)/shard_map/all_to_all | solution.py:170
  40.0 4.8 %all-to-all-start.1 = ((bf16[32,384,128]{2,1,0:T(8,128)(2,1)}), bf16[32,384,128]{2,1,0:T(8,128)(2,1)}, u32[]{:S(2)}, u32[]{:S(2)}) async-start(bf16[32,384,128]{2,1,0:T(8,128)(2,1)} %apply_tiles.3), calls=%async_computation.1 | async-start | bytes 6291456 | tf_op jit(solution)/shard_map/all_to_all | solution.py:172
  44.8 0.1 pad_add_fusion.spot_ref
  44.9 1.5 %fusion.cols_ref = s32[32]{0:T(128)S(1)} fusion(bf16[32,144,128]{2,1,0:T(8,128)(2,1)} %all-to-all-done.sent_ref), kind=kLoop, calls=%fused_computation.2 | loop fusion | flops 32 | bytes 192 | tf_op jit(solution)/shard_map/convert_element_type | solution.py:173
  46.4 43.1 %all-to-all-done.1.sent_ref = bf16[32,384,128]{2,1,0:T(8,128)(2,1)} async-done(((bf16[32,384,128]{2,1,0:T(8,128)(2,1)}), bf16[32,384,128]{2,1,0:T(8,128)(2,1)}, u32[]{:S(2)}, u32[]{:S(2)}) %all-to-all-start.1) | async-done | bytes 3145760 | tf_op jit(solution)/shard_map/all_to_all | solution.py:172
  89.5 0.0 copy-done
  89.5 5.1 %join.3 = (f32[24,8,512]{2,1,0:T(8,128)S(1)}, f32[24,8,512]{2,1,0:T(8,128)S(1)}) custom-call(s32[2]{0:T(128)S(1)} %pad_add_fusion.spot_ref, s32[32]{0:T(128)S(1)} %fusion.cols_ref, bf16[24,128,512]{2,1,0:T(8,128)(2,1)S(1)} %bitcast.10, bf16[32,384,128]{2,1,0:T(8,128)(2,1)} %all-to-all-done.1.sent_ref), custom_call_target="tpu_custom_call" | custom-call | flops 1610612736 | bytes 7864320 | tf_op jit(solution)/shard_map/join/pallas_call | solution.py:122
  94.6 2.8 %collective-permute-start.1 = (f32[24,8,512]{2,1,0:T(8,128)S(1)}, f32[24,8,512]{2,1,0:T(8,128)S(1)}, u32[]{:S(2)}, u32[]{:S(2)}) collective-permute-start(f32[24,8,512]{2,1,0:T(8,128)S(1)} %get-tuple-element.12), channel_id=1, source_target_pairs={{0,1},{1,0},{2,3},{3,2},{4,5},{5,4},{6,7},{7,6},{8,9},{9,8},{10,11... | collective-permute-start | bytes 1179656 | tf_op jit(solution)/shard_map/ppermute | solution.py:179
  97.4 3.7 %join.2 = (f32[8,8,512]{2,1,0:T(8,128)S(1)}, f32[8,8,512]{2,1,0:T(8,128)S(1)}) custom-call(s32[2]{0:T(128)S(1)} %pad_add_fusion.spot_ref, s32[32]{0:T(128)S(1)} %fusion.cols_ref, bf16[24,128,512]{2,1,0:T(8,128)(2,1)S(1)} %bitcast.11, bf16[32,144,128]{2,1,0:T(8,128)(2,1)} %all-to-all-done.sent_ref), custom_call_target="tpu_custom_call" | custom-call | flops 536870912 | bytes 4849664 | tf_op jit(solution)/shard_map/join/pallas_call | solution.py:122
  101.2 0.1 collective-permute-start
  101.3 1.3 %collective-permute-done = f32[8,8,512]{2,1,0:T(8,128)S(1)} collective-permute-done((f32[8,8,512]{2,1,0:T(8,128)S(1)}, f32[8,8,512]{2,1,0:T(8,128)S(1)}, u32[]{:S(2)}, u32[]{:S(2)}) %collective-permute-start) | collective-permute-done | bytes 131104 | tf_op jit(solution)/shard_map/ppermute | solution.py:178
  102.6 0.0 collective-permute-done.1
  102.6 0.1 add.49
  102.7 0.8 pad_maximum_fusion
  103.5 3.9 %all-to-all-start.2 = ((f32[32,8,512]{2,1,0:T(8,128)}), f32[32,8,512]{2,1,0:T(8,128)S(1)}, u32[]{:S(2)}, u32[]{:S(2)}) async-start(f32[32,8,512]{2,1,0:T(8,128)} %pad_maximum_fusion), calls=%async_computation.2 | async-start | bytes 1048576 | tf_op jit(solution)/shard_map/all_to_all | solution.py:183
  107.5 11.6 %all-to-all-done.2 = f32[32,8,512]{2,1,0:T(8,128)S(1)} async-done(((f32[32,8,512]{2,1,0:T(8,128)}), f32[32,8,512]{2,1,0:T(8,128)S(1)}, u32[]{:S(2)}, u32[]{:S(2)}) %all-to-all-start.2) | async-done | bytes 524320 | tf_op jit(solution)/shard_map/all_to_all | solution.py:183
  119.1 3.1 %collective-permute-start.2 = (f32[2,512]{1,0:T(2,128)S(1)}, f32[2,512]{1,0:T(2,128)S(1)}, u32[]{:S(2)}, u32[]{:S(2)}) collective-permute-start(f32[2,512]{1,0:T(2,128)S(1)} %get-tuple-element.13), channel_id=1, source_target_pairs={{0,2},{1,3},{2,4},{3,5},{4,6},{5,7},{6,0},{7,1},{8,10},{9,11},{10,... | collective-permute-start | bytes 12296 | tf_op jit(solution)/shard_map/ppermute | solution.py:192
  122.2 2.2 %collective-permute-start.4 = (f32[2,512]{1,0:T(2,128)S(1)}, f32[2,512]{1,0:T(2,128)S(1)}, u32[]{:S(2)}, u32[]{:S(2)}) collective-permute-start(f32[2,512]{1,0:T(2,128)S(1)} %get-tuple-element.14), channel_id=1, source_target_pairs={{0,6},{1,7},{2,0},{3,1},{4,2},{5,3},{6,4},{7,5},{8,14},{9,15},{10,... | collective-permute-start | bytes 12296 | tf_op jit(solution)/shard_map/ppermute | solution.py:192
  124.4 4.4 %collective-permute-start.3 = (f32[2,512]{1,0:T(2,128)S(1)}, f32[2,512]{1,0:T(2,128)S(1)}, u32[]{:S(2)}, u32[]{:S(2)}) collective-permute-start(f32[2,512]{1,0:T(2,128)S(1)} %get-tuple-element.15), channel_id=1, source_target_pairs={{0,4},{1,5},{2,6},{3,7},{4,0},{5,1},{6,2},{7,3},{8,12},{9,13},{10,... | collective-permute-start | bytes 12296 | tf_op jit(solution)/shard_map/ppermute | solution.py:192
  128.8 0.0 collective-permute-done.2
  128.8 0.0 collective-permute-done.4
  128.8 2.0 %collective-permute-done.3 = f32[2,512]{1,0:T(2,128)S(1)} collective-permute-done((f32[2,512]{1,0:T(2,128)S(1)}, f32[2,512]{1,0:T(2,128)S(1)}, u32[]{:S(2)}, u32[]{:S(2)}) %collective-permute-start.3) | collective-permute-done | bytes 4128 | tf_op jit(solution)/shard_map/ppermute | solution.py:192
  130.8 0.6 add_multiply_fusion
  (3 shorter events, 0.1 us)
Async XLA Ops:
  12.5 27.5 %all-to-all-start = ((bf16[32,144,128]{2,1,0:T(8,128)(2,1)}), bf16[32,144,128]{2,1,0:T(8,128)(2,1)}, u32[]{:S(2)}, u32[]{:S(2)}) async-start(bf16[32,144,128]{2,1,0:T(8,128)(2,1)} %apply_tiles.2), calls=%async_computation | async-start | bytes 2359296 | tf_op jit(solution)/shard_map/all_to_all | solution.py:170
  35.5 54.0 %copy-start = (bf16[3072,512]{1,0:T(8,128)(2,1)S(1)}, bf16[3072,512]{1,0:T(8,128)(2,1)}, u32[]{:S(2)}) copy-start(bf16[3072,512]{1,0:T(8,128)(2,1)} %param.5) | copy-start | bytes 9437188
  40.0 49.5 %all-to-all-start.1 = ((bf16[32,384,128]{2,1,0:T(8,128)(2,1)}), bf16[32,384,128]{2,1,0:T(8,128)(2,1)}, u32[]{:S(2)}, u32[]{:S(2)}) async-start(bf16[32,384,128]{2,1,0:T(8,128)(2,1)} %apply_tiles.3), calls=%async_computation.1 | async-start | bytes 6291456 | tf_op jit(solution)/shard_map/all_to_all | solution.py:172
  94.6 8.0 %collective-permute-start.1 = (f32[24,8,512]{2,1,0:T(8,128)S(1)}, f32[24,8,512]{2,1,0:T(8,128)S(1)}, u32[]{:S(2)}, u32[]{:S(2)}) collective-permute-start(f32[24,8,512]{2,1,0:T(8,128)S(1)} %get-tuple-element.12), channel_id=1, source_target_pairs={{0,1},{1,0},{2,3},{3,2},{4,5},{5,4},{6,7},{7,6},{8,9},{9,8},{10,11... | collective-permute-start | bytes 1179656 | tf_op jit(solution)/shard_map/ppermute | solution.py:179
  101.2 1.4 %collective-permute-start = (f32[8,8,512]{2,1,0:T(8,128)S(1)}, f32[8,8,512]{2,1,0:T(8,128)S(1)}, u32[]{:S(2)}, u32[]{:S(2)}) collective-permute-start(f32[8,8,512]{2,1,0:T(8,128)S(1)} %get-tuple-element.10), channel_id=1, source_target_pairs={{0,1},{1,0},{2,3},{3,2},{4,5},{5,4},{6,7},{7,6},{8,9},{9,8},{10,11... | collective-permute-start | bytes 393224 | tf_op jit(solution)/shard_map/ppermute | solution.py:178
  103.5 15.5 %all-to-all-start.2 = ((f32[32,8,512]{2,1,0:T(8,128)}), f32[32,8,512]{2,1,0:T(8,128)S(1)}, u32[]{:S(2)}, u32[]{:S(2)}) async-start(f32[32,8,512]{2,1,0:T(8,128)} %pad_maximum_fusion), calls=%async_computation.2 | async-start | bytes 1048576 | tf_op jit(solution)/shard_map/all_to_all | solution.py:183
  119.1 9.7 %collective-permute-start.2 = (f32[2,512]{1,0:T(2,128)S(1)}, f32[2,512]{1,0:T(2,128)S(1)}, u32[]{:S(2)}, u32[]{:S(2)}) collective-permute-start(f32[2,512]{1,0:T(2,128)S(1)} %get-tuple-element.13), channel_id=1, source_target_pairs={{0,2},{1,3},{2,4},{3,5},{4,6},{5,7},{6,0},{7,1},{8,10},{9,11},{10,... | collective-permute-start | bytes 12296 | tf_op jit(solution)/shard_map/ppermute | solution.py:192
  122.2 6.6 %collective-permute-start.4 = (f32[2,512]{1,0:T(2,128)S(1)}, f32[2,512]{1,0:T(2,128)S(1)}, u32[]{:S(2)}, u32[]{:S(2)}) collective-permute-start(f32[2,512]{1,0:T(2,128)S(1)} %get-tuple-element.14), channel_id=1, source_target_pairs={{0,6},{1,7},{2,0},{3,1},{4,2},{5,3},{6,4},{7,5},{8,14},{9,15},{10,... | collective-permute-start | bytes 12296 | tf_op jit(solution)/shard_map/ppermute | solution.py:192
  124.4 6.4 %collective-permute-start.3 = (f32[2,512]{1,0:T(2,128)S(1)}, f32[2,512]{1,0:T(2,128)S(1)}, u32[]{:S(2)}, u32[]{:S(2)}) collective-permute-start(f32[2,512]{1,0:T(2,128)S(1)} %get-tuple-element.15), channel_id=1, source_target_pairs={{0,4},{1,5},{2,6},{3,7},{4,0},{5,1},{6,2},{7,3},{8,12},{9,13},{10,... | collective-permute-start | bytes 12296 | tf_op jit(solution)/shard_map/ppermute | solution.py:192

commit v3 on v2

v3 whole, which is shorter than its diff:
```python
import functools
import math

import jax
import jax.numpy as jnp
from jax import lax
from jax.experimental import pallas as pl
from jax.experimental.pallas import tpu as pltpu
from jax.sharding import PartitionSpec as P


discount = 0.95
extra_rows = 16
peers_per_step = 8


def dot(left, right):
    return jnp.dot(left, right, preferred_element_type=jnp.float32)


def apply_kernel(rows_ref, counts_ref, cols_ref, tiles_ref, phi_ref, out_ref, turned):
    step = pl.program_id(0)
    block_count, features, _ = turned.shape
    peers, use_count = tiles_ref.shape[:2]

    @pl.when(step == 0)
    def _():
        def turn(b, carry):
            for k in range(2):
                turned[2 * b + k] = phi_ref[2 * b + k].T
            return carry

        lax.fori_loop(0, block_count // 2, turn, 0)

    for local in range(peers):
        peer = step * peers + local
        count = counts_ref[peer]
        left = jnp.concatenate([turned[rows_ref[u, peer]] for u in range(use_count)], axis=1)
        right = jnp.concatenate(
            [
                jnp.where(u < count, tiles_ref[local, u], jnp.zeros((), tiles_ref.dtype))
                for u in range(use_count)
            ],
            axis=0,
        )
        product = dot(left, right) * (-discount)
        out_ref[local, :features] = product.astype(out_ref.dtype)
        column = jnp.full((extra_rows, out_ref.shape[2]), cols_ref[peer], jnp.int32)
        out_ref[local, features:] = column.astype(jnp.float32).astype(out_ref.dtype)


def apply_tiles(rows, counts, cols, tiles, blocks):
    peers, use_count, tile_size, _ = tiles.shape
    block_count, _, features = blocks.shape
    height = features + extra_rows
    per_step = peers_per_step
    return pl.pallas_call(
        apply_kernel,
        out_shape=jax.ShapeDtypeStruct((peers, height, tile_size), jnp.bfloat16),
        grid_spec=pltpu.PrefetchScalarGridSpec(
            num_scalar_prefetch=3,
            grid=(peers // per_step,),
            in_specs=[
                pl.BlockSpec(
                    (per_step, use_count, tile_size, tile_size), lambda p, *_: (p, 0, 0, 0)
                ),
                pl.BlockSpec((block_count, tile_size, features), lambda p, *_: (0, 0, 0)),
            ],
            out_specs=pl.BlockSpec((per_step, height, tile_size), lambda p, *_: (p, 0, 0)),
            scratch_shapes=[pltpu.VMEM((block_count, features, tile_size), jnp.bfloat16)],
        ),
        cost_estimate=pl.CostEstimate(
            flops=2 * peers * use_count * tile_size * tile_size * features,
            bytes_accessed=2 * (tiles.size + blocks.size + peers * height * tile_size),
            transcendentals=0,
        ),
        name="apply_tiles",
    )(rows, counts, cols, tiles, blocks)


def halves(total, own_one):
    height, features = total.shape
    rows = total.reshape(height // 16, 2, 8, features)
    even, odd = rows[:, 0], rows[:, 1]
    place = lax.broadcasted_iota(jnp.int32, even.shape, 1)
    lower = lax.rem(place, 4) < 2
    zero = jnp.where(lower, even, jnp.roll(odd, 2, axis=1))
    one = jnp.where(lower, jnp.roll(even, -2, axis=1), odd)
    return jnp.where(own_one, one, zero), jnp.where(own_one, zero, one)


def gram_kernel(spot_ref, phi_ref, out_ref):
    depth, tile_size, features = phi_ref.shape
    tall = phi_ref[...].reshape(depth * tile_size, features)
    total = lax.dot_general(
        tall, tall, (((0,), (0,)), ((), ())), preferred_element_type=jnp.float32
    )
    out_ref[...] = halves(total, spot_ref[1] == 1)[0]


def gram_rows(spot, blocks, depth):
    _, tile_size, features = blocks.shape
    return pl.pallas_call(
        gram_kernel,
        out_shape=jax.ShapeDtypeStruct((features // 16, 8, features), jnp.float32),
        grid_spec=pltpu.PrefetchScalarGridSpec(
            num_scalar_prefetch=1,
            grid=(1,),
            in_specs=[
                pl.BlockSpec((depth, tile_size, features), lambda p, spot_ref: (spot_ref[0], 0, 0))
            ],
            out_specs=pl.BlockSpec((features // 16, 8, features), lambda p, *_: (0, 0, 0)),
        ),
        compiler_params=pltpu.CompilerParams(vmem_limit_bytes=16 << 20),
        cost_estimate=pl.CostEstimate(
            flops=2 * depth * tile_size * features * features,
            bytes_accessed=2 * depth * tile_size * features + 2 * features * features,
            transcendentals=0,
        ),
        name="gram_rows",
    )(spot, blocks)


def join_kernel(spot_ref, phi_ref, sent_ref, keep_ref, give_ref, total):
    step = pl.program_id(0)
    height, _ = total.shape
    peers = sent_ref.shape[0]

    @pl.when(step == 0)
    def _():
        total[...] = jnp.zeros_like(total)

    wanted = [
        jnp.max(sent_ref[s, height:].astype(jnp.float32)).astype(jnp.int32) for s in range(peers)
    ]
    left = jnp.concatenate([sent_ref[s, :height] for s in range(peers)], axis=1)
    right = jnp.concatenate([phi_ref[w] for w in wanted], axis=0)
    total[...] += dot(left, right)

    @pl.when(step == pl.num_programs(0) - 1)
    def _():
        keep, give = halves(total[...], spot_ref[1] == 1)
        keep_ref[...] = keep
        give_ref[...] = give


def join(spot, blocks, sent, per_step=8):
    peers, height, tile_size = sent.shape
    block_count, _, features = blocks.shape
    half = jax.ShapeDtypeStruct((features // 16, 8, features), jnp.float32)
    return pl.pallas_call(
        join_kernel,
        out_shape=(half, half),
        grid_spec=pltpu.PrefetchScalarGridSpec(
            num_scalar_prefetch=1,
            grid=(peers // per_step,),
            in_specs=[
                pl.BlockSpec((block_count, tile_size, features), lambda p, *_: (0, 0, 0)),
                pl.BlockSpec((per_step, height, tile_size), lambda p, *_: (p, 0, 0)),
            ],
            out_specs=[
                pl.BlockSpec((features // 16, 8, features), lambda p, *_: (0, 0, 0)),
                pl.BlockSpec((features // 16, 8, features), lambda p, *_: (0, 0, 0)),
            ],
            scratch_shapes=[pltpu.VMEM((features, features), jnp.float32)],
        ),
        compiler_params=pltpu.CompilerParams(vmem_limit_bytes=24 << 20),
        cost_estimate=pl.CostEstimate(
            flops=2 * peers * tile_size * features * features,
            bytes_accessed=2 * (blocks.size + sent.size) + 8 * features * features,
            transcendentals=0,
        ),
        name="join",
    )(spot, blocks, sent)


def body(basis_rows, tile_blocks, tile_cols, tile_rows, tile_counts):
    shards = lax.axis_size("state")
    groups = lax.axis_size("group")
    local_rows, features = basis_rows.shape
    tile_size = tile_blocks.shape[-1]
    block_count = local_rows // tile_size
    blocks = basis_rows.reshape(block_count, tile_size, features)
    exchange = functools.partial(
        lax.all_to_all, axis_name="state", split_axis=0, concat_axis=0, tiled=True
    )
    swap = [(g, g ^ 1) for g in range(groups)]
    member = lax.axis_index("group")
    spot = jnp.stack([member >> 1, member & 1]).astype(jnp.int32)

    sent = apply_tiles(
        tile_rows[0, 0].T, tile_counts[0, 0], tile_cols[0, 0], tile_blocks[0, 0], blocks
    )
    got = exchange(sent)
    gram = gram_rows(spot, blocks, 2 * block_count // groups)
    keep, give = join(spot, blocks, got)
    half = (keep + gram) + lax.ppermute(give, "group", swap)
    owned = exchange(half).sum(0)

    quads = groups // 2
    quad = member >> 1
    final = lax.dynamic_slice_in_dim(owned, 2 * place_of(quad), 2, 0)
    for shift in range(1, quads):
        target = lax.rem(quad + shift, quads)
        piece = lax.dynamic_slice_in_dim(owned, 2 * place_of(target), 2, 0)
        ring = [(g, (g + 2 * shift) % groups) for g in range(groups)]
        final = final + lax.ppermute(piece, "group", ring)
    return final * (1.0 / math.sqrt(local_rows * shards))


def place_of(quad):
    return (quad & 1) * 2 + (quad >> 1)


def solution(mesh):
    in_specs = (
        P("state", None),
        P("state", "group", None, None, None, None),
        P("state", "group", None),
        P("state", "group", None, None),
        P("state", "group", None),
    )
    out_specs = P(("state", "group"), None)
    return jax.shard_map(body, mesh=mesh, in_specs=in_specs, out_specs=out_specs, check_vma=False)
```

time: 133 us -> 130 us (0.977)
  waiting for transfers between devices: 62.4 us -> 82.7 us
  Pallas kernels: 33.6 us -> 20 us
  starting transfers between devices: 30.6 us -> 23.5 us
  other arithmetic: 3.13 us -> 1.67 us
    all_to_all x2 -> x1, waiting for transfers between devices: 47.6 us -> 67.6 us  [body(): got = exchange(sent)]
    pallas_call x4 -> x3, Pallas kernels: 33.6 us -> 20 us  [the longest x1 13 us: apply_tiles(): pl.pallas_call(apply_kernel, out_shape=jax.ShapeDtypeStruct((peers, heigh...]
    all_to_all x2 -> x1, starting transfers between devices: 14.1 us -> 9.59 us  [body(): got = exchange(sent)]
    convert_element_type x1 -> x0, other arithmetic: 1.5 us -> none  [body(): wanted = got_one[:, first_features, 0].astype(jnp.int32)]
    ppermute x2 -> x1, starting transfers between devices: 2.89 us -> 1.64 us  [body(): half = keep + gram + lax.ppermute(give, 'group', swap)]
  transfers between devices with their start and end apart: 8 -> 6, of which waited for: 5 -> 4; matrix products, arithmetic and copies ran while one was open for 1% -> 0% of each run, Pallas kernels for 13% -> 1%
where the time goes in v3:
time: 130 us; the launch traced here: 129 us
  waiting for transfers between devices  82.7 us (64%)
  starting transfers between devices  23.5 us (18%)
  Pallas kernels  20 us (15%)
  other arithmetic  1.67 us (1%)
    all_to_all x1, waiting for transfers between devices, body(): got = exchange(sent)  67.6 us
    pallas_call x1, Pallas kernels, apply_tiles(): pl.pallas_call(apply_kernel, out_shape=jax.ShapeDtypeStruct((peers, heigh...  13 us
    all_to_all x1, waiting for transfers between devices, body(): owned = exchange(half).sum(0)  11.6 us
    all_to_all x1, starting transfers between devices, body(): got = exchange(sent)  9.59 us
    ppermute x3, starting transfers between devices, body(): final = final + lax.ppermute(piece, 'group', ring)  8.43 us
    pallas_call x1, Pallas kernels, join(): pl.pallas_call(join_kernel, out_shape=(half, half), grid_spec=pltpu.Prefe...  5.89 us
    all_to_all x1, starting transfers between devices, body(): owned = exchange(half).sum(0)  3.89 us
    ppermute x3, waiting for transfers between devices, body(): final = final + lax.ppermute(piece, 'group', ring)  3.11 us
  transfers between devices with their start and end apart: 6, of which 4 were waited for; matrix products, arithmetic and copies ran while one was open for 0% of the time, Pallas kernels for 1%

profile of v3, /device:TPU:1, one launch (start us, length us, event | category | flops | bytes accessed | tf_op | source)
XLA Modules:
  0.0 129.4 jit_solution(3382704613010136962)
XLA Ops:
  0.0 1.3 copy.8
  1.3 13.0 %apply_tiles.1 = bf16[32,528,128]{2,1,0:T(8,128)(2,1)} custom-call(s32[6,32]{1,0:T(8,128)} %bitcast.15, s32[32]{0:T(128)} %bitcast.16, s32[32]{0:T(128)} %bitcast.17, bf16[32,6,128,128]{3,2,1,0:T(8,128)(2,1)} %bitcast.14, bf16[24,128,512]{2,1,0:T(8,128)(2,1)} %bitcast.11), custom_call_target="tpu_custom_call" | custom-call | flops 3221225472 | bytes 13762560 | tf_op jit(solution)/shard_map/apply_tiles/pallas_call | solution.py:57
  14.3 0.0 copy-start
  14.3 9.6 %all-to-all-start = ((bf16[32,528,128]{2,1,0:T(8,128)(2,1)}), bf16[32,528,128]{2,1,0:T(8,128)(2,1)}, u32[]{:S(2)}, u32[]{:S(2)}) async-start(bf16[32,528,128]{2,1,0:T(8,128)(2,1)} %apply_tiles.1), calls=%async_computation | async-start | bytes 8650752 | tf_op jit(solution)/shard_map/all_to_all | solution.py:194
  23.9 0.1 pad_add_fusion.spot_ref
  24.0 67.6 %all-to-all-done.sent_ref = bf16[32,528,128]{2,1,0:T(8,128)(2,1)} async-done(((bf16[32,528,128]{2,1,0:T(8,128)(2,1)}), bf16[32,528,128]{2,1,0:T(8,128)(2,1)}, u32[]{:S(2)}, u32[]{:S(2)}) %all-to-all-start) | async-done | bytes 4325408 | tf_op jit(solution)/shard_map/all_to_all | solution.py:194
  91.6 0.0 copy-done
  91.6 5.9 %join.1 = (f32[32,8,512]{2,1,0:T(8,128)S(1)}, f32[32,8,512]{2,1,0:T(8,128)S(1)}) custom-call(s32[2]{0:T(128)S(1)} %pad_add_fusion.spot_ref, bf16[24,128,512]{2,1,0:T(8,128)(2,1)S(1)} %bitcast.12, bf16[32,528,128]{2,1,0:T(8,128)(2,1)} %all-to-all-done.sent_ref), custom_call_target="tpu_custom_call" | custom-call | flops 2147483648 | bytes 9568256 | tf_op jit(solution)/shard_map/join/pallas_call | solution.py:151
  97.5 1.6 %collective-permute-start = (f32[32,8,512]{2,1,0:T(8,128)S(1)}, f32[32,8,512]{2,1,0:T(8,128)S(1)}, u32[]{:S(2)}, u32[]{:S(2)}) collective-permute-start(f32[32,8,512]{2,1,0:T(8,128)S(1)} %get-tuple-element.8), channel_id=1, source_target_pairs={{0,1},{1,0},{2,3},{3,2},{4,5},{5,4},{6,7},{7,6},{8,9},{9,8},{10,11... | collective-permute-start | bytes 1572872 | tf_op jit(solution)/shard_map/ppermute | solution.py:197
  99.1 1.1 gram_rows.1
  100.3 0.4 collective-permute-done
  100.7 0.9 add_add_fusion
  101.6 3.9 %all-to-all-start.1 = ((f32[32,8,512]{2,1,0:T(8,128)}), f32[32,8,512]{2,1,0:T(8,128)S(1)}, u32[]{:S(2)}, u32[]{:S(2)}) async-start(f32[32,8,512]{2,1,0:T(8,128)} %add_add_fusion), calls=%async_computation.1 | async-start | bytes 1048576 | tf_op jit(solution)/shard_map/all_to_all | solution.py:198
  105.6 11.6 %all-to-all-done.1 = f32[32,8,512]{2,1,0:T(8,128)S(1)} async-done(((f32[32,8,512]{2,1,0:T(8,128)}), f32[32,8,512]{2,1,0:T(8,128)S(1)}, u32[]{:S(2)}, u32[]{:S(2)}) %all-to-all-start.1) | async-done | bytes 524320 | tf_op jit(solution)/shard_map/all_to_all | solution.py:198
  117.2 5.2 %collective-permute-start.3 = (f32[2,512]{1,0:T(2,128)S(1)}, f32[2,512]{1,0:T(2,128)S(1)}, u32[]{:S(2)}, u32[]{:S(2)}) collective-permute-start(f32[2,512]{1,0:T(2,128)S(1)} %get-tuple-element.10), channel_id=1, source_target_pairs={{0,6},{1,7},{2,0},{3,1},{4,2},{5,3},{6,4},{7,5},{8,14},{9,15},{10,... | collective-permute-start | bytes 12296 | tf_op jit(solution)/shard_map/ppermute | solution.py:207
  122.4 1.2 collective-permute-start.2
  123.6 2.1 %collective-permute-start.1 = (f32[2,512]{1,0:T(2,128)S(1)}, f32[2,512]{1,0:T(2,128)S(1)}, u32[]{:S(2)}, u32[]{:S(2)}) collective-permute-start(f32[2,512]{1,0:T(2,128)S(1)} %get-tuple-element.9), channel_id=1, source_target_pairs={{0,2},{1,3},{2,4},{3,5},{4,6},{5,7},{6,0},{7,1},{8,10},{9,11},{10,... | collective-permute-start | bytes 12296 | tf_op jit(solution)/shard_map/ppermute | solution.py:207
  125.7 0.0 collective-permute-done.3
  125.7 3.1 %collective-permute-done.2 = f32[2,512]{1,0:T(2,128)S(1)} collective-permute-done((f32[2,512]{1,0:T(2,128)S(1)}, f32[2,512]{1,0:T(2,128)S(1)}, u32[]{:S(2)}, u32[]{:S(2)}) %collective-permute-start.2) | collective-permute-done | bytes 4128 | tf_op jit(solution)/shard_map/ppermute | solution.py:207
  128.8 0.0 collective-permute-done.1
  128.8 0.6 add_multiply_fusion
  (2 shorter events, 0.1 us)
Async XLA Ops:
  14.3 77.3 %copy-start = (bf16[3072,512]{1,0:T(8,128)(2,1)S(1)}, bf16[3072,512]{1,0:T(8,128)(2,1)}, u32[]{:S(2)}) copy-start(bf16[3072,512]{1,0:T(8,128)(2,1)} %param.5) | copy-start | bytes 9437188
  14.3 77.3 %all-to-all-start = ((bf16[32,528,128]{2,1,0:T(8,128)(2,1)}), bf16[32,528,128]{2,1,0:T(8,128)(2,1)}, u32[]{:S(2)}, u32[]{:S(2)}) async-start(bf16[32,528,128]{2,1,0:T(8,128)(2,1)} %apply_tiles.1), calls=%async_computation | async-start | bytes 8650752 | tf_op jit(solution)/shard_map/all_to_all | solution.py:194
  97.5 3.2 %collective-permute-start = (f32[32,8,512]{2,1,0:T(8,128)S(1)}, f32[32,8,512]{2,1,0:T(8,128)S(1)}, u32[]{:S(2)}, u32[]{:S(2)}) collective-permute-start(f32[32,8,512]{2,1,0:T(8,128)S(1)} %get-tuple-element.8), channel_id=1, source_target_pairs={{0,1},{1,0},{2,3},{3,2},{4,5},{5,4},{6,7},{7,6},{8,9},{9,8},{10,11... | collective-permute-start | bytes 1572872 | tf_op jit(solution)/shard_map/ppermute | solution.py:197
  101.6 15.5 %all-to-all-start.1 = ((f32[32,8,512]{2,1,0:T(8,128)}), f32[32,8,512]{2,1,0:T(8,128)S(1)}, u32[]{:S(2)}, u32[]{:S(2)}) async-start(f32[32,8,512]{2,1,0:T(8,128)} %add_add_fusion), calls=%async_computation.1 | async-start | bytes 1048576 | tf_op jit(solution)/shard_map/all_to_all | solution.py:198
  117.2 8.4 %collective-permute-start.3 = (f32[2,512]{1,0:T(2,128)S(1)}, f32[2,512]{1,0:T(2,128)S(1)}, u32[]{:S(2)}, u32[]{:S(2)}) collective-permute-start(f32[2,512]{1,0:T(2,128)S(1)} %get-tuple-element.10), channel_id=1, source_target_pairs={{0,6},{1,7},{2,0},{3,1},{4,2},{5,3},{6,4},{7,5},{8,14},{9,15},{10,... | collective-permute-start | bytes 12296 | tf_op jit(solution)/shard_map/ppermute | solution.py:207
  122.4 6.4 %collective-permute-start.2 = (f32[2,512]{1,0:T(2,128)S(1)}, f32[2,512]{1,0:T(2,128)S(1)}, u32[]{:S(2)}, u32[]{:S(2)}) collective-permute-start(f32[2,512]{1,0:T(2,128)S(1)} %get-tuple-element.11), channel_id=1, source_target_pairs={{0,4},{1,5},{2,6},{3,7},{4,0},{5,1},{6,2},{7,3},{8,12},{9,13},{10,... | collective-permute-start | bytes 12296 | tf_op jit(solution)/shard_map/ppermute | solution.py:207
  123.6 5.2 %collective-permute-start.1 = (f32[2,512]{1,0:T(2,128)S(1)}, f32[2,512]{1,0:T(2,128)S(1)}, u32[]{:S(2)}, u32[]{:S(2)}) collective-permute-start(f32[2,512]{1,0:T(2,128)S(1)} %get-tuple-element.9), channel_id=1, source_target_pairs={{0,2},{1,3},{2,4},{3,5},{4,6},{5,7},{6,0},{7,1},{8,10},{9,11},{10,... | collective-permute-start | bytes 12296 | tf_op jit(solution)/shard_map/ppermute | solution.py:207

commit v4 on v3

--- a/solution.py
+++ b/solution.py
@@ -10,7 +10,7 @@
 
 
 discount = 0.95
-extra_rows = 16
+extra_rows = 8
 peers_per_step = 8
 
 
@@ -18,33 +18,25 @@
     return jnp.dot(left, right, preferred_element_type=jnp.float32)
 
 
-def apply_kernel(rows_ref, counts_ref, cols_ref, tiles_ref, phi_ref, out_ref, turned):
+def apply_kernel(rows_ref, counts_ref, cols_ref, tiles_ref, phi_ref, out_ref):
     step = pl.program_id(0)
-    block_count, features, _ = turned.shape
-    peers, use_count = tiles_ref.shape[:2]
-
-    @pl.when(step == 0)
-    def _():
-        def turn(b, carry):
-            for k in range(2):
-                turned[2 * b + k] = phi_ref[2 * b + k].T
-            return carry
-
-        lax.fori_loop(0, block_count // 2, turn, 0)
-
+    peers, use_count, tile_size, _ = tiles_ref.shape
+    features = phi_ref.shape[2]
     for local in range(peers):
         peer = step * peers + local
         count = counts_ref[peer]
-        left = jnp.concatenate([turned[rows_ref[u, peer]] for u in range(use_count)], axis=1)
-        right = jnp.concatenate(
+        left = jnp.concatenate(
             [
-                jnp.where(u < count, tiles_ref[local, u], jnp.zeros((), tiles_ref.dtype))
+                jnp.where(u < count, tiles_ref[local, u], jnp.zeros((), tiles_ref.dtype)).T
                 for u in range(use_count)
             ],
-            axis=0,
+            axis=1,
         )
-        product = dot(left, right) * (-discount)
-        out_ref[local, :features] = product.astype(out_ref.dtype)
+        right = jnp.concatenate([phi_ref[rows_ref[u, 0, peer]] for u in range(use_count)], axis=0)
+        product = (dot(left, right) * (-discount)).astype(out_ref.dtype)
+        for part in range(features // tile_size):
+            span = pl.ds(part * tile_size, tile_size)
+            out_ref[local, span] = product[:, part * tile_size : (part + 1) * tile_size]
         column = jnp.full((extra_rows, out_ref.shape[2]), cols_ref[peer], jnp.int32)
         out_ref[local, features:] = column.astype(jnp.float32).astype(out_ref.dtype)
 
@@ -67,7 +59,6 @@
                 pl.BlockSpec((block_count, tile_size, features), lambda p, *_: (0, 0, 0)),
             ],
             out_specs=pl.BlockSpec((per_step, height, tile_size), lambda p, *_: (p, 0, 0)),
-            scratch_shapes=[pltpu.VMEM((block_count, features, tile_size), jnp.bfloat16)],
         ),
         cost_estimate=pl.CostEstimate(
             flops=2 * peers * use_count * tile_size * tile_size * features,
@@ -133,7 +124,20 @@
     wanted = [
         jnp.max(sent_ref[s, height:].astype(jnp.float32)).astype(jnp.int32) for s in range(peers)
     ]
-    left = jnp.concatenate([sent_ref[s, :height] for s in range(peers)], axis=1)
+    tile_size = sent_ref.shape[2]
+    left = jnp.concatenate(
+        [
+            jnp.concatenate(
+                [
+                    sent_ref[s, pl.ds(part * tile_size, tile_size)].T
+                    for part in range(height // tile_size)
+                ],
+                axis=0,
+            )
+            for s in range(peers)
+        ],
+        axis=1,
+    )
     right = jnp.concatenate([phi_ref[w] for w in wanted], axis=0)
     total[...] += dot(left, right)
 
@@ -176,7 +180,7 @@
 
 def body(basis_rows, tile_blocks, tile_cols, tile_rows, tile_counts):
     shards = lax.axis_size("state")
-    groups = lax.axis_size("group")
+    quads = lax.axis_size("quad")
     local_rows, features = basis_rows.shape
     tile_size = tile_blocks.shape[-1]
     block_count = local_rows // tile_size
@@ -184,27 +188,29 @@
     exchange = functools.partial(
         lax.all_to_all, axis_name="state", split_axis=0, concat_axis=0, tiled=True
     )
-    swap = [(g, g ^ 1) for g in range(groups)]
-    member = lax.axis_index("group")
-    spot = jnp.stack([member >> 1, member & 1]).astype(jnp.int32)
+    spot = jnp.stack([lax.axis_index("quad"), lax.axis_index("core")]).astype(jnp.int32)
 
     sent = apply_tiles(
-        tile_rows[0, 0].T, tile_counts[0, 0], tile_cols[0, 0], tile_blocks[0, 0], blocks
-    )
+        tile_rows[0].transpose(2, 0, 1),
+        tile_counts[0, 0],
+        tile_cols[0, 0],
+        tile_blocks[0, 0],
+        blocks,
+    )
+    quad = lax.axis_index("quad")
+    starts = [2 * place_of(lax.rem(quad + shift, quads)) for shift in range(quads)]
+    sent, spot, starts = lax.optimization_barrier((sent, spot, starts))
     got = exchange(sent)
-    gram = gram_rows(spot, blocks, 2 * block_count // groups)
     keep, give = join(spot, blocks, got)
-    half = (keep + gram) + lax.ppermute(give, "group", swap)
-    owned = exchange(half).sum(0)
-
-    quads = groups // 2
-    quad = member >> 1
-    final = lax.dynamic_slice_in_dim(owned, 2 * place_of(quad), 2, 0)
+    taken = lax.ppermute(give, "core", [(0, 1), (1, 0)])
+    gram = gram_rows(spot, blocks, block_count // quads)
+    owned = exchange((keep + gram) + taken).sum(0)
+
+    pieces = [lax.dynamic_slice_in_dim(owned, start, 2, 0) for start in starts]
+    final = pieces[0]
     for shift in range(1, quads):
-        target = lax.rem(quad + shift, quads)
-        piece = lax.dynamic_slice_in_dim(owned, 2 * place_of(target), 2, 0)
-        ring = [(g, (g + 2 * shift) % groups) for g in range(groups)]
-        final = final + lax.ppermute(piece, "group", ring)
+        ring = [(q, (q + shift) % quads) for q in range(quads)]
+        final = final + lax.ppermute(pieces[shift], "quad", ring)
     return final * (1.0 / math.sqrt(local_rows * shards))
 
 
@@ -213,12 +219,17 @@
 
 
 def solution(mesh):
+    shards, groups = mesh.devices.shape
+    fine = jax.sharding.Mesh(
+        mesh.devices.reshape(shards, groups // 2, 2), ("state", "quad", "core")
+    )
+    group = ("quad", "core")
     in_specs = (
         P("state", None),
-        P("state", "group", None, None, None, None),
-        P("state", "group", None),
-        P("state", "group", None, None),
-        P("state", "group", None),
-    )
-    out_specs = P(("state", "group"), None)
-    return jax.shard_map(body, mesh=mesh, in_specs=in_specs, out_specs=out_specs, check_vma=False)
+        P("state", group, None, None, None, None),
+        P("state", group, None),
+        P("state", group, None, None),
+        P("state", group, None),
+    )
+    out_specs = P(("state",) + group, None)
+    return jax.shard_map(body, mesh=fine, in_specs=in_specs, out_specs=out_specs, check_vma=False)

time: 130 us -> 108 us (0.83)
  waiting for transfers between devices: 82.7 us -> 13.8 us
  blocking collectives: 0 us -> 60.9 us
  starting transfers between devices: 23.5 us -> 15.7 us
  Pallas kernels: 20 us -> 14.5 us
    all_to_all x2 -> x1, waiting for transfers between devices: 79.3 us -> 11.4 us  [body(): owned = exchange(keep + gram + taken).sum(0)]
    all_to_all x0 -> x1, blocking collectives: none -> 60.9 us  [body(): got = exchange(sent)]
    all_to_all x2 -> x1, starting transfers between devices: 13.5 us -> 3.89 us  [body(): owned = exchange(keep + gram + taken).sum(0)]
    pallas_call x1, Pallas kernels: 13 us -> 9.12 us  [apply_tiles(): pl.pallas_call(apply_kernel, out_shape=jax.ShapeDtypeStruct((peers, heigh...]
    ppermute x4, starting transfers between devices: 10.1 us -> 11.8 us  [the longest x3 9.67 us: body(): final = final + lax.ppermute(pieces[shift], 'quad', ring)]
    pallas_call x1, Pallas kernels: 5.89 us -> 4.28 us  [join(): pl.pallas_call(join_kernel, out_shape=(half, half), grid_spec=pltpu.Prefe...]
  transfers between devices with their start and end apart: 6 -> 5, of which waited for: 4 -> 3; matrix products, arithmetic and copies ran while one was open for 0% -> 0% of each run, Pallas kernels for 1% -> 1%
where the time goes in v4:
time: 108 us; the launch traced here: 107 us
  blocking collectives  60.9 us (56%)
  starting transfers between devices  15.7 us (15%)
  Pallas kernels  14.5 us (13%)
  waiting for transfers between devices  13.8 us (13%)
  other arithmetic  1.66 us (2%)
    all_to_all x1, blocking collectives, body(): got = exchange(sent)  60.9 us
    all_to_all x1, waiting for transfers between devices, body(): owned = exchange(keep + gram + taken).sum(0)  11.4 us
    ppermute x3, starting transfers between devices, body(): final = final + lax.ppermute(pieces[shift], 'quad', ring)  9.67 us
    pallas_call x1, Pallas kernels, apply_tiles(): pl.pallas_call(apply_kernel, out_shape=jax.ShapeDtypeStruct((peers, heigh...  9.12 us
    pallas_call x1, Pallas kernels, join(): pl.pallas_call(join_kernel, out_shape=(half, half), grid_spec=pltpu.Prefe...  4.28 us
    all_to_all x1, starting transfers between devices, body(): owned = exchange(keep + gram + taken).sum(0)  3.89 us
    ppermute x1, starting transfers between devices, body(): taken = lax.ppermute(give, 'core', [(0, 1), (1, 0)])  2.18 us
  transfers between devices with their start and end apart: 5, of which 3 were waited for; matrix products, arithmetic and copies ran while one was open for 0% of the time, Pallas kernels for 1%

profile of v4, /device:TPU:1, one launch (start us, length us, event | category | flops | bytes accessed | tf_op | source)
XLA Modules:
  0.0 106.7 jit_solution(8144532940893241343)
XLA Ops:
  0.0 0.1 pad_add_fusion.spot_ref
  0.1 9.1 %apply_tiles.1 = bf16[32,520,128]{2,1,0:T(8,128)(2,1)} custom-call(s32[6,1,32]{2,1,0:T(1,128)} %bitcast.13, s32[32]{0:T(128)} %bitcast.14, s32[32]{0:T(128)} %bitcast.15, bf16[32,6,128,128]{3,2,1,0:T(8,128)(2,1)} %bitcast.12, bf16[24,128,512]{2,1,0:T(8,128)(2,1)} %bitcast.9), custom_call_target="tpu_custom_call" | custom-call | flops 3221225472 | bytes 13697024 | tf_op jit(solution)/shard_map/apply_tiles/pallas_call | solution.py:49
  9.2 0.0 copy-start
  9.2 60.9 %all_to_all.10.sent_ref = bf16[32,520,128]{2,1,0:T(8,128)(2,1)S(1)} all-to-all(bf16[32,520,128]{2,1,0:T(8,128)(2,1)} %apply_tiles.1), channel_id=1, replica_groups=mesh['state'=32,'quad'=4,'core'=2] {'state'}, dimensions={0} | all-to-all | bytes 8519680 | tf_op jit(solution)/shard_map/all_to_all | solution.py:203
  70.1 0.0 copy-done
  70.1 4.3 %join.1 = (f32[32,8,512]{2,1,0:T(8,128)S(1)}, f32[32,8,512]{2,1,0:T(8,128)S(1)}) custom-call(s32[2]{0:T(128)S(1)} %pad_add_fusion.spot_ref, bf16[24,128,512]{2,1,0:T(8,128)(2,1)S(1)} %bitcast.10, bf16[32,520,128]{2,1,0:T(8,128)(2,1)S(1)} %all_to_all.10.sent_ref), custom_call_target="tpu_custom_call" | custom-call | flops 2147483648 | bytes 9502720 | tf_op jit(solution)/shard_map/join/pallas_call | solution.py:155
  74.4 2.2 %collective-permute-start = (f32[32,8,512]{2,1,0:T(8,128)S(1)}, f32[32,8,512]{2,1,0:T(8,128)S(1)}, u32[]{:S(2)}, u32[]{:S(2)}) collective-permute-start(f32[32,8,512]{2,1,0:T(8,128)S(1)} %get-tuple-element.16), channel_id=1, source_target_pairs={{0,1},{1,0},{2,3},{3,2},{4,5},{5,4},{6,7},{7,6},{8,9},{9,8},{10,11... | collective-permute-start | bytes 1572872 | tf_op jit(solution)/shard_map/ppermute | solution.py:205
  76.6 1.1 %gram_rows.1 = f32[32,8,512]{2,1,0:T(8,128)S(1)} custom-call(s32[2]{0:T(128)S(1)} %pad_add_fusion.spot_ref, bf16[24,128,512]{2,1,0:T(8,128)(2,1)S(1)} %bitcast.11), custom_call_target="tpu_custom_call" | custom-call | flops 402653184 | bytes 1310720 | tf_op jit(solution)/shard_map/gram_rows/pallas_call | solution.py:94
  77.7 0.4 collective-permute-done
  78.1 0.9 add_add_fusion
  79.0 3.9 %all-to-all-start.1 = ((f32[32,8,512]{2,1,0:T(8,128)}), f32[32,8,512]{2,1,0:T(8,128)S(1)}, u32[]{:S(2)}, u32[]{:S(2)}) async-start(f32[32,8,512]{2,1,0:T(8,128)} %add_add_fusion), calls=%async_computation.1 | async-start | bytes 1048576 | tf_op jit(solution)/shard_map/all_to_all | solution.py:207
  83.0 11.4 %all-to-all-done.1 = f32[32,8,512]{2,1,0:T(8,128)S(1)} async-done(((f32[32,8,512]{2,1,0:T(8,128)}), f32[32,8,512]{2,1,0:T(8,128)S(1)}, u32[]{:S(2)}, u32[]{:S(2)}) %all-to-all-start.1) | async-done | bytes 524320 | tf_op jit(solution)/shard_map/all_to_all | solution.py:207
  94.5 3.1 %collective-permute-start.1 = (f32[2,512]{1,0:T(2,128)S(1)}, f32[2,512]{1,0:T(2,128)S(1)}, u32[]{:S(2)}, u32[]{:S(2)}) collective-permute-start(f32[2,512]{1,0:T(2,128)S(1)} %get-tuple-element.21), channel_id=1, source_target_pairs={{0,2},{2,4},{4,6},{6,0},{1,3},{3,5},{5,7},{7,1},{8,10},{10,12},{12... | collective-permute-start | bytes 12296 | tf_op jit(solution)/shard_map/ppermute | solution.py:213
  97.5 2.2 %collective-permute-start.3 = (f32[2,512]{1,0:T(2,128)S(1)}, f32[2,512]{1,0:T(2,128)S(1)}, u32[]{:S(2)}, u32[]{:S(2)}) collective-permute-start(f32[2,512]{1,0:T(2,128)S(1)} %get-tuple-element.22), channel_id=1, source_target_pairs={{0,6},{2,0},{4,2},{6,4},{1,7},{3,1},{5,3},{7,5},{8,14},{10,8},{12,... | collective-permute-start | bytes 12296 | tf_op jit(solution)/shard_map/ppermute | solution.py:213
  99.7 4.4 %collective-permute-start.2 = (f32[2,512]{1,0:T(2,128)S(1)}, f32[2,512]{1,0:T(2,128)S(1)}, u32[]{:S(2)}, u32[]{:S(2)}) collective-permute-start(f32[2,512]{1,0:T(2,128)S(1)} %get-tuple-element.23), channel_id=1, source_target_pairs={{0,4},{2,6},{4,0},{6,2},{1,5},{3,7},{5,1},{7,3},{8,12},{10,14},{12... | collective-permute-start | bytes 12296 | tf_op jit(solution)/shard_map/ppermute | solution.py:213
  104.1 0.0 collective-permute-done.1
  104.1 0.0 collective-permute-done.3
  104.1 2.0 %collective-permute-done.2 = f32[2,512]{1,0:T(2,128)S(1)} collective-permute-done((f32[2,512]{1,0:T(2,128)S(1)}, f32[2,512]{1,0:T(2,128)S(1)}, u32[]{:S(2)}, u32[]{:S(2)}) %collective-permute-start.2) | collective-permute-done | bytes 4128 | tf_op jit(solution)/shard_map/ppermute | solution.py:213
  106.1 0.6 add_multiply_fusion
  (2 shorter events, 0.1 us)
Async XLA Ops:
  9.2 60.9 %copy-start = (bf16[3072,512]{1,0:T(8,128)(2,1)S(1)}, bf16[3072,512]{1,0:T(8,128)(2,1)}, u32[]{:S(2)}) copy-start(bf16[3072,512]{1,0:T(8,128)(2,1)} %param.5) | copy-start | bytes 9437188
  74.4 3.7 %collective-permute-start = (f32[32,8,512]{2,1,0:T(8,128)S(1)}, f32[32,8,512]{2,1,0:T(8,128)S(1)}, u32[]{:S(2)}, u32[]{:S(2)}) collective-permute-start(f32[32,8,512]{2,1,0:T(8,128)S(1)} %get-tuple-element.16), channel_id=1, source_target_pairs={{0,1},{1,0},{2,3},{3,2},{4,5},{5,4},{6,7},{7,6},{8,9},{9,8},{10,11... | collective-permute-start | bytes 1572872 | tf_op jit(solution)/shard_map/ppermute | solution.py:205
  79.0 15.4 %all-to-all-start.1 = ((f32[32,8,512]{2,1,0:T(8,128)}), f32[32,8,512]{2,1,0:T(8,128)S(1)}, u32[]{:S(2)}, u32[]{:S(2)}) async-start(f32[32,8,512]{2,1,0:T(8,128)} %add_add_fusion), calls=%async_computation.1 | async-start | bytes 1048576 | tf_op jit(solution)/shard_map/all_to_all | solution.py:207
  94.5 9.7 %collective-permute-start.1 = (f32[2,512]{1,0:T(2,128)S(1)}, f32[2,512]{1,0:T(2,128)S(1)}, u32[]{:S(2)}, u32[]{:S(2)}) collective-permute-start(f32[2,512]{1,0:T(2,128)S(1)} %get-tuple-element.21), channel_id=1, source_target_pairs={{0,2},{2,4},{4,6},{6,0},{1,3},{3,5},{5,7},{7,1},{8,10},{10,12},{12... | collective-permute-start | bytes 12296 | tf_op jit(solution)/shard_map/ppermute | solution.py:213
  97.5 6.6 %collective-permute-start.3 = (f32[2,512]{1,0:T(2,128)S(1)}, f32[2,512]{1,0:T(2,128)S(1)}, u32[]{:S(2)}, u32[]{:S(2)}) collective-permute-start(f32[2,512]{1,0:T(2,128)S(1)} %get-tuple-element.22), channel_id=1, source_target_pairs={{0,6},{2,0},{4,2},{6,4},{1,7},{3,1},{5,3},{7,5},{8,14},{10,8},{12,... | collective-permute-start | bytes 12296 | tf_op jit(solution)/shard_map/ppermute | solution.py:213
  99.7 6.4 %collective-permute-start.2 = (f32[2,512]{1,0:T(2,128)S(1)}, f32[2,512]{1,0:T(2,128)S(1)}, u32[]{:S(2)}, u32[]{:S(2)}) collective-permute-start(f32[2,512]{1,0:T(2,128)S(1)} %get-tuple-element.23), channel_id=1, source_target_pairs={{0,4},{2,6},{4,0},{6,2},{1,5},{3,7},{5,1},{7,3},{8,12},{10,14},{12... | collective-permute-start | bytes 12296 | tf_op jit(solution)/shard_map/ppermute | solution.py:213

commit v5 on v4

v5 whole, which is shorter than its diff:
```python
import functools
import math

import jax
import jax.numpy as jnp
from jax import lax
from jax.experimental import pallas as pl
from jax.experimental.pallas import tpu as pltpu
from jax.sharding import PartitionSpec as P


discount = 0.95
extra_rows = 8
peers_per_step = 16
peers_per_dot = 8


def dot(left, right):
    return jnp.dot(left, right, preferred_element_type=jnp.float32)


def apply_kernel(rows_ref, counts_ref, cols_ref, tiles_ref, phi_ref, out_ref):
    step = pl.program_id(0)
    peers, use_count, tile_size, _ = tiles_ref.shape
    features = phi_ref.shape[2]
    for local in range(peers):
        peer = step * peers + local
        count = counts_ref[peer]
        left = jnp.concatenate(
            [
                jnp.where(u < count, tiles_ref[local, u], jnp.zeros((), tiles_ref.dtype)).T
                for u in range(use_count)
            ],
            axis=1,
        )
        right = jnp.concatenate([phi_ref[rows_ref[u, 0, peer]] for u in range(use_count)], axis=0)
        product = (dot(left, right) * (-discount)).astype(out_ref.dtype)
        for part in range(features // tile_size):
            span = pl.ds(part * tile_size, tile_size)
            out_ref[local, span] = product[:, part * tile_size : (part + 1) * tile_size]
        column = jnp.full((extra_rows, out_ref.shape[2]), cols_ref[peer], jnp.int32)
        out_ref[local, features:] = column.astype(jnp.float32).astype(out_ref.dtype)


def apply_tiles(rows, counts, cols, tiles, blocks):
    peers, use_count, tile_size, _ = tiles.shape
    block_count, _, features = blocks.shape
    height = features + extra_rows
    per_step = peers_per_step
    return pl.pallas_call(
        apply_kernel,
        out_shape=jax.ShapeDtypeStruct((peers, height, tile_size), jnp.bfloat16),
        grid_spec=pltpu.PrefetchScalarGridSpec(
            num_scalar_prefetch=3,
            grid=(peers // per_step,),
            in_specs=[
                pl.BlockSpec(
                    (per_step, use_count, tile_size, tile_size), lambda p, *_: (p, 0, 0, 0)
                ),
                pl.BlockSpec((block_count, tile_size, features), lambda p, *_: (0, 0, 0)),
            ],
            out_specs=pl.BlockSpec((per_step, height, tile_size), lambda p, *_: (p, 0, 0)),
        ),
        cost_estimate=pl.CostEstimate(
            flops=2 * peers * use_count * tile_size * tile_size * features,
            bytes_accessed=2 * (tiles.size + blocks.size + peers * height * tile_size),
            transcendentals=0,
        ),
        name="apply_tiles",
    )(rows, counts, cols, tiles, blocks)


def store_half(total_ref, core, out_ref):
    parts, height, _ = total_ref.shape
    for k in range(2):
        for part in range(parts):
            rows = total_ref[part, pl.ds(core * 2 + k, height // 4, stride=4), :]
            out_ref[pl.ds(k * parts + part, height // 4, stride=2 * parts), :] = rows


def gram_kernel(spot_ref, phi_ref, out_ref, total):
    depth, tile_size, features = phi_ref.shape
    tall = phi_ref[...].reshape(depth * tile_size, features)
    product = lax.dot_general(
        tall, tall, (((0,), (0,)), ((), ())), preferred_element_type=jnp.float32
    )
    parts, _, lanes = total.shape
    for part in range(parts):
        total[part] = product[:, part * lanes : (part + 1) * lanes]
    store_half(total, spot_ref[1], out_ref)


def gram_rows(spot, blocks, depth):
    _, tile_size, features = blocks.shape
    return pl.pallas_call(
        gram_kernel,
        out_shape=jax.ShapeDtypeStruct((features * features // 256, 128), jnp.float32),
        grid_spec=pltpu.PrefetchScalarGridSpec(
            num_scalar_prefetch=1,
            grid=(1,),
            in_specs=[
                pl.BlockSpec((depth, tile_size, features), lambda p, spot_ref: (spot_ref[0], 0, 0))
            ],
            out_specs=pl.BlockSpec((features * features // 256, 128), lambda p, *_: (0, 0)),
            scratch_shapes=[pltpu.VMEM((features // 128, features, 128), jnp.float32)],
        ),
        compiler_params=pltpu.CompilerParams(vmem_limit_bytes=16 << 20),
        cost_estimate=pl.CostEstimate(
            flops=2 * depth * tile_size * features * features,
            bytes_accessed=2 * depth * tile_size * features + 2 * features * features,
            transcendentals=0,
        ),
        name="gram_rows",
    )(spot, blocks)


def join_kernel(spot_ref, phi_ref, sent_ref, keep_ref, give_ref, total):
    parts, height, lanes = total.shape
    peers = sent_ref.shape[0]
    wanted = [
        jnp.max(sent_ref[s, height:].astype(jnp.float32)).astype(jnp.int32) for s in range(peers)
    ]
    for first in range(0, peers, peers_per_dot):
        group = range(first, first + peers_per_dot)
        left = jnp.concatenate(
            [
                jnp.concatenate(
                    [sent_ref[s, pl.ds(part * lanes, lanes)].T for part in range(parts)], axis=0
                )
                for s in group
            ],
            axis=1,
        )
        right = jnp.concatenate([phi_ref[wanted[s]] for s in group], axis=0)
        product = dot(left, right)
        for part in range(parts):
            piece = product[:, part * lanes : (part + 1) * lanes]
            total[part] = piece if first == 0 else total[part] + piece
    store_half(total, spot_ref[1], keep_ref)
    store_half(total, 1 - spot_ref[1], give_ref)


def join(spot, blocks, sent):
    peers, _, tile_size = sent.shape
    _, _, features = blocks.shape
    half = jax.ShapeDtypeStruct((features * features // 256, 128), jnp.float32)
    whole = pl.BlockSpec(memory_space=pltpu.VMEM)
    return pl.pallas_call(
        join_kernel,
        out_shape=(half, half),
        in_specs=[pl.BlockSpec(memory_space=pltpu.SMEM), whole, whole],
        out_specs=[whole, whole],
        scratch_shapes=[pltpu.VMEM((features // 128, features, 128), jnp.float32)],
        compiler_params=pltpu.CompilerParams(vmem_limit_bytes=24 << 20),
        cost_estimate=pl.CostEstimate(
            flops=2 * peers * tile_size * features * features,
            bytes_accessed=2 * (blocks.size + sent.size) + 8 * features * features,
            transcendentals=0,
        ),
        name="join",
    )(spot, blocks, sent)


def body(basis_rows, tile_blocks, tile_cols, tile_rows, tile_counts):
    shards = lax.axis_size(("xy", "zl"))
    quads = lax.axis_size("quad")
    local_rows, features = basis_rows.shape
    tile_size = tile_blocks.shape[-1]
    block_count = local_rows // tile_size
    blocks = basis_rows.reshape(block_count, tile_size, features)
    exchange = functools.partial(
        lax.all_to_all, split_axis=0, concat_axis=0, tiled=True
    )
    spot = jnp.stack([lax.axis_index("quad"), lax.axis_index("core")]).astype(jnp.int32)

    sent = apply_tiles(
        tile_rows[0].transpose(2, 0, 1),
        tile_counts[0, 0],
        tile_cols[0, 0],
        tile_blocks[0, 0],
        blocks,
    )
    sent, spot = lax.optimization_barrier((sent, spot))
    got = exchange(sent, ("xy", "zl"))
    keep, give = join(spot, blocks, got)
    taken = lax.ppermute(give, "core", [(0, 1), (1, 0)])
    gram = gram_rows(spot, blocks, block_count // quads)
    half = ((keep + gram) + taken).reshape(shards // 2, -1, tile_size)
    owned = exchange(half, "xy").sum(0)
    owned = exchange(owned.reshape(2 * quads, -1, tile_size), ("zl", "quad")).sum(0)
    return owned.reshape(-1, features) * (1.0 / math.sqrt(local_rows * shards))


def solution(mesh):
    shards, groups = mesh.devices.shape
    fine = jax.sharding.Mesh(
        mesh.devices.reshape(shards // 2, 2, groups // 2, 2), ("xy", "zl", "quad", "core")
    )
    group = ("quad", "core")
    in_specs = (
        P(("xy","zl"), None),
        P(("xy","zl"), group, None, None, None, None),
        P(("xy","zl"), group, None),
        P(("xy","zl"), group, None, None),
        P(("xy","zl"), group, None),
    )
    out_specs = P(("xy","zl") + group, None)
    return jax.shard_map(body, mesh=fine, in_specs=in_specs, out_specs=out_specs, check_vma=False)
```

time: 108 us -> 106 us (0.981)
  blocking collectives: 60.9 us -> 88.2 us
  waiting for transfers between devices: 13.8 us -> 0.25 us
  starting transfers between devices: 15.7 us -> 2.18 us
  other arithmetic: 1.66 us -> 0.2 us
  Pallas kernels: 14.5 us -> 13.4 us
    all_to_all x1 -> x3, blocking collectives: 60.9 us -> 88.2 us  [the longest x1 60.9 us: body(): got = exchange(sent, ('xy', 'zl'))]
    all_to_all x1 -> x0, waiting for transfers between devices: 11.4 us -> none  [body(): owned = exchange(keep + gram + taken).sum(0)]
    ppermute x3 -> x0, starting transfers between devices: 9.67 us -> none  [body(): final = final + lax.ppermute(pieces[shift], 'quad', ring)]
    all_to_all x1 -> x0, starting transfers between devices: 3.89 us -> none  [body(): owned = exchange(keep + gram + taken).sum(0)]
    ppermute x3 -> x0, waiting for transfers between devices: 2 us -> none  [body(): final = final + lax.ppermute(pieces[shift], 'quad', ring)]
  transfers between devices with their start and end apart: 5 -> 1, of which waited for: 3 -> 1; matrix products, arithmetic and copies ran while one was open for 0% -> 0% of each run, Pallas kernels for 1% -> 1%
where the time goes in v5:
time: 106 us; the launch traced here: 105 us
  blocking collectives  88.2 us (83%)
  Pallas kernels  13.4 us (13%)
  starting transfers between devices  2.18 us (2%)
    all_to_all x1, blocking collectives, body(): got = exchange(sent, ('xy', 'zl'))  60.9 us
    all_to_all x1, blocking collectives, body(): owned = exchange(half, 'xy').sum(0)  13.7 us
    all_to_all x1, blocking collectives, body(): exchange(owned.reshape(2 * quads, -1, tile_size), ('zl', 'quad')).sum(0)  13.7 us
    pallas_call x1, Pallas kernels, apply_tiles(): pl.pallas_call(apply_kernel, out_shape=jax.ShapeDtypeStruct((peers, heigh...  8.62 us
    pallas_call x1, Pallas kernels, join(): pl.pallas_call(join_kernel, out_shape=(half, half), in_specs=[pl.BlockSpe...  3.49 us
    ppermute x1, starting transfers between devices, body(): taken = lax.ppermute(give, 'core', [(0, 1), (1, 0)])  2.18 us
  transfers between devices with their start and end apart: 1, of which 1 were waited for; matrix products, arithmetic and copies ran while one was open for 0% of the time, Pallas kernels for 1%

profile of v5, /device:TPU:1, one launch (start us, length us, event | category | flops | bytes accessed | tf_op | source)
XLA Modules:
  0.0 104.9 jit_solution(17969691887217190136)
XLA Ops:
  0.0 0.1 pad_add_fusion.spot_ref
  0.1 8.6 %apply_tiles.1 = bf16[32,520,128]{2,1,0:T(8,128)(2,1)} custom-call(s32[6,1,32]{2,1,0:T(1,128)} %bitcast.17, s32[32]{0:T(128)} %bitcast.18, s32[32]{0:T(128)} %bitcast.19, bf16[32,6,128,128]{3,2,1,0:T(8,128)(2,1)} %bitcast.14, bf16[24,128,512]{2,1,0:T(8,128)(2,1)} %bitcast.11), custom_call_target="tpu_custom_call" | custom-call | flops 3221225472 | bytes 13697024 | tf_op jit(solution)/shard_map/apply_tiles/pallas_call | solution.py:50
  8.7 0.0 copy-start
  8.7 60.9 %all_to_all.15.sent_ref = bf16[32,520,128]{2,1,0:T(8,128)(2,1)S(1)} all-to-all(bf16[32,520,128]{2,1,0:T(8,128)(2,1)} %apply_tiles.1), channel_id=1, replica_groups=mesh['xy'=16,'zl'=2,'quad'=4,'core'=2] {'xy','zl'}, dimensions={0} | all-to-all | bytes 8519680 | tf_op jit(solution)/shard_map/all_to_all | solution.py:184
  69.6 0.0 copy-done
  69.6 3.5 %join.1 = (f32[1024,128]{1,0:T(8,128)S(1)}, f32[1024,128]{1,0:T(8,128)S(1)}) custom-call(s32[2]{0:T(128)S(1)} %pad_add_fusion.spot_ref, bf16[24,128,512]{2,1,0:T(8,128)(2,1)S(1)} %bitcast.12, bf16[32,520,128]{2,1,0:T(8,128)(2,1)S(1)} %all_to_all.15.sent_ref), custom_call_target="tpu_custom_call" | custom-call | flops 2147483648 | bytes 9502720 | tf_op jit(solution)/shard_map/join/pallas_call | solution.py:148
  73.1 2.2 %collective-permute-start = (f32[1024,128]{1,0:T(8,128)S(1)}, f32[1024,128]{1,0:T(8,128)S(1)}, u32[]{:S(2)}, u32[]{:S(2)}) collective-permute-start(f32[1024,128]{1,0:T(8,128)S(1)} %get-tuple-element.12), channel_id=1, source_target_pairs={{0,1},{1,0},{2,3},{3,2},{4,5},{5,4},{6,7},{7,6},{8,9},{9,8},{10,11... | collective-permute-start | bytes 1572872 | tf_op jit(solution)/shard_map/ppermute | solution.py:186
  75.3 1.3 %gram_rows.1 = f32[1024,128]{1,0:T(8,128)S(1)} custom-call(s32[2]{0:T(128)S(1)} %pad_add_fusion.spot_ref, bf16[24,128,512]{2,1,0:T(8,128)(2,1)S(1)} %bitcast.13), custom_call_target="tpu_custom_call" | custom-call | flops 402653184 | bytes 1310720 | tf_op jit(solution)/shard_map/gram_rows/pallas_call | solution.py:95
  76.6 0.2 collective-permute-done
  76.8 0.1 add_add_fusion
  76.9 13.7 %all_to_all.16 = f32[16,64,128]{2,1,0:T(8,128)S(1)} all-to-all(f32[16,64,128]{2,1,0:T(8,128)S(1)} %bitcast.15), channel_id=1, replica_groups=mesh['xy'=16,'zl'=2,'quad'=4,'core'=2] {'xy'}, dimensions={0} | all-to-all | bytes 1048576 | tf_op jit(solution)/shard_map/all_to_all | solution.py:189
  90.6 13.7 %all_to_all.17 = f32[8,8,128]{2,1,0:T(8,128)S(1)} all-to-all(f32[8,8,128]{2,1,0:T(8,128)S(1)} %bitcast.16), channel_id=1, replica_groups=mesh['xy'=16,'zl'=2,'quad'=4,'core'=2] {'zl','quad'}, dimensions={0} | all-to-all | bytes 65536 | tf_op jit(solution)/shard_map/all_to_all | solution.py:190
  104.3 0.6 mul.11
  (3 shorter events, 0.1 us)
Async XLA Ops:
  8.7 60.9 %copy-start = (bf16[3072,512]{1,0:T(8,128)(2,1)S(1)}, bf16[3072,512]{1,0:T(8,128)(2,1)}, u32[]{:S(2)}) copy-start(bf16[3072,512]{1,0:T(8,128)(2,1)} %param.5) | copy-start | bytes 9437188
  73.1 3.7 %collective-permute-start = (f32[1024,128]{1,0:T(8,128)S(1)}, f32[1024,128]{1,0:T(8,128)S(1)}, u32[]{:S(2)}, u32[]{:S(2)}) collective-permute-start(f32[1024,128]{1,0:T(8,128)S(1)} %get-tuple-element.12), channel_id=1, source_target_pairs={{0,1},{1,0},{2,3},{3,2},{4,5},{5,4},{6,7},{7,6},{8,9},{9,8},{10,11... | collective-permute-start | bytes 1572872 | tf_op jit(solution)/shard_map/ppermute | solution.py:186

commit v6 on v5

--- a/solution.py
+++ b/solution.py
@@ -11,7 +11,7 @@
 
 discount = 0.95
 extra_rows = 8
-peers_per_step = 16
+tile_groups = 4
 peers_per_dot = 8
 
 
@@ -19,55 +19,78 @@
     return jnp.dot(left, right, preferred_element_type=jnp.float32)
 
 
-def apply_kernel(rows_ref, counts_ref, cols_ref, tiles_ref, phi_ref, out_ref):
-    step = pl.program_id(0)
-    peers, use_count, tile_size, _ = tiles_ref.shape
-    features = phi_ref.shape[2]
-    for local in range(peers):
-        peer = step * peers + local
-        count = counts_ref[peer]
-        left = jnp.concatenate(
-            [
-                jnp.where(u < count, tiles_ref[local, u], jnp.zeros((), tiles_ref.dtype)).T
-                for u in range(use_count)
-            ],
-            axis=1,
-        )
-        right = jnp.concatenate([phi_ref[rows_ref[u, 0, peer]] for u in range(use_count)], axis=0)
-        product = (dot(left, right) * (-discount)).astype(out_ref.dtype)
-        for part in range(features // tile_size):
-            span = pl.ds(part * tile_size, tile_size)
-            out_ref[local, span] = product[:, part * tile_size : (part + 1) * tile_size]
-        column = jnp.full((extra_rows, out_ref.shape[2]), cols_ref[peer], jnp.int32)
-        out_ref[local, features:] = column.astype(jnp.float32).astype(out_ref.dtype)
+def apply_kernel(
+    rows_ref, counts_ref, cols_ref, tiles_hbm, phi_hbm, out, tiles, phi, tile_sems, phi_sem
+):
+    peers, use_count, tile_size, _ = tiles.shape
+    features = phi.shape[2]
+    groups = tile_sems.shape[0]
+    size = peers // groups
+    spans = [pl.ds(i * size, size) for i in range(groups)]
+    load_phi = pltpu.make_async_copy(phi_hbm, phi, phi_sem)
+    loads = [
+        pltpu.make_async_copy(tiles_hbm.at[spans[i]], tiles.at[spans[i]], tile_sems.at[i])
+        for i in range(groups)
+    ]
+    load_phi.start()
+    loads[0].start()
+    loads[1].start()
+    load_phi.wait()
+    for i in range(2, groups):
+        loads[i].start()
+    for i in range(groups):
+        loads[i].wait()
+        for peer in range(i * size, (i + 1) * size):
+            count = counts_ref[peer]
+            left = jnp.concatenate(
+                [
+                    jnp.where(u < count, tiles[peer, u], jnp.zeros((), tiles.dtype)).T
+                    for u in range(use_count)
+                ],
+                axis=1,
+            )
+            right = jnp.concatenate([phi[rows_ref[u, 0, peer]] for u in range(use_count)], axis=0)
+            product = (dot(left, right) * (-discount)).astype(out.dtype)
+            for part in range(features // tile_size):
+                span = pl.ds(part * tile_size, tile_size)
+                out[peer, span] = product[:, part * tile_size : (part + 1) * tile_size]
+            column = jnp.full((extra_rows, tile_size), cols_ref[peer], jnp.int32)
+            out[peer, features:] = column.astype(jnp.float32).astype(out.dtype)
 
 
 def apply_tiles(rows, counts, cols, tiles, blocks):
     peers, use_count, tile_size, _ = tiles.shape
-    block_count, _, features = blocks.shape
-    height = features + extra_rows
-    per_step = peers_per_step
+    _, _, features = blocks.shape
+    result = jax.ShapeDtypeStruct((peers, features + extra_rows, tile_size), jnp.bfloat16)
+    there = pl.BlockSpec(memory_space=pl.ANY)
     return pl.pallas_call(
         apply_kernel,
-        out_shape=jax.ShapeDtypeStruct((peers, height, tile_size), jnp.bfloat16),
+        out_shape=result,
         grid_spec=pltpu.PrefetchScalarGridSpec(
             num_scalar_prefetch=3,
-            grid=(peers // per_step,),
-            in_specs=[
-                pl.BlockSpec(
-                    (per_step, use_count, tile_size, tile_size), lambda p, *_: (p, 0, 0, 0)
-                ),
-                pl.BlockSpec((block_count, tile_size, features), lambda p, *_: (0, 0, 0)),
+            grid=(1,),
+            in_specs=[there, there],
+            out_specs=pl.BlockSpec(memory_space=pltpu.VMEM),
+            scratch_shapes=[
+                pltpu.VMEM(tiles.shape, tiles.dtype),
+                pltpu.VMEM(blocks.shape, blocks.dtype),
+                pltpu.SemaphoreType.DMA((tile_groups,)),
+                pltpu.SemaphoreType.DMA,
             ],
-            out_specs=pl.BlockSpec((per_step, height, tile_size), lambda p, *_: (p, 0, 0)),
-        ),
+        ),
+        compiler_params=pltpu.CompilerParams(vmem_limit_bytes=24 << 20),
         cost_estimate=pl.CostEstimate(
             flops=2 * peers * use_count * tile_size * tile_size * features,
-            bytes_accessed=2 * (tiles.size + blocks.size + peers * height * tile_size),
+            bytes_accessed=2 * (tiles.size + blocks.size + result.size),
             transcendentals=0,
         ),
         name="apply_tiles",
-    )(rows, counts, cols, tiles, blocks)
+    )(
+        *[
+            pltpu.with_memory_space_constraint(array, pltpu.HBM)
+            for array in (rows, counts, cols, tiles, blocks)
+        ]
+    )
 
 
 def store_half(total_ref, core, out_ref):
@@ -75,7 +98,7 @@
     for k in range(2):
         for part in range(parts):
             rows = total_ref[part, pl.ds(core * 2 + k, height // 4, stride=4), :]
-            out_ref[pl.ds(k * parts + part, height // 4, stride=2 * parts), :] = rows
+            out_ref[pl.ds(2 * part + k, height // 4, stride=2 * parts), :] = rows
 
 
 def gram_kernel(spot_ref, phi_ref, out_ref, total):
@@ -188,6 +211,7 @@
     half = ((keep + gram) + taken).reshape(shards // 2, -1, tile_size)
     owned = exchange(half, "xy").sum(0)
     owned = exchange(owned.reshape(2 * quads, -1, tile_size), ("zl", "quad")).sum(0)
+    owned = owned.reshape(-1, 2, tile_size).transpose(1, 0, 2)
     return owned.reshape(-1, features) * (1.0 / math.sqrt(local_rows * shards))
 
 

time: 106 us -> 105 us (level)
  Pallas kernels: 13.4 us -> 12 us
    pallas_call x1, Pallas kernels: 8.62 us -> 7.24 us  [apply_tiles(): pl.pallas_call(apply_kernel, out_shape=result, grid_spec=pltpu.PrefetchSc...]
where the time goes in v6:
time: 105 us; the launch traced here: 103 us
  blocking collectives  88.1 us (84%)
  Pallas kernels  12 us (11%)
  starting transfers between devices  2.17 us (2%)
    all_to_all x1, blocking collectives, body(): got = exchange(sent, ('xy', 'zl'))  60.7 us
    all_to_all x1, blocking collectives, body(): owned = exchange(half, 'xy').sum(0)  13.7 us
    all_to_all x1, blocking collectives, body(): exchange(owned.reshape(2 * quads, -1, tile_size), ('zl', 'quad')).sum(0)  13.7 us
    pallas_call x1, Pallas kernels, apply_tiles(): pl.pallas_call(apply_kernel, out_shape=result, grid_spec=pltpu.PrefetchSc...  7.24 us
    pallas_call x1, Pallas kernels, join(): pl.pallas_call(join_kernel, out_shape=(half, half), in_specs=[pl.BlockSpe...  3.49 us
    ppermute x1, starting transfers between devices, body(): taken = lax.ppermute(give, 'core', [(0, 1), (1, 0)])  2.17 us
  transfers between devices with their start and end apart: 1, of which 1 were waited for; matrix products, arithmetic and copies ran while one was open for 0% of the time, Pallas kernels for 1%

profile of v6, /device:TPU:1, one launch (start us, length us, event | category | flops | bytes accessed | tf_op | source)
XLA Modules:
  0.0 103.3 jit_solution(11200823098074418002)
XLA Ops:
  0.0 0.1 pad_add_fusion.spot_ref
  0.1 7.2 %apply_tiles.1 = bf16[32,520,128]{2,1,0:T(8,128)(2,1)S(1)} custom-call(s32[6,1,32]{2,1,0:T(1,128)} %bitcast.22, s32[32]{0:T(128)} %bitcast.23, s32[32]{0:T(128)} %bitcast.24, bf16[32,6,128,128]{3,2,1,0:T(8,128)(2,1)} %bitcast.19, bf16[24,128,512]{2,1,0:T(8,128)(2,1)} %bitcast.16), custom_call_target="tpu_custom_call" | custom-call | flops 3221225472 | bytes 13697024 | tf_op jit(solution)/shard_map/apply_tiles/pallas_call | solution.py:66
  7.3 0.0 copy-start
  7.3 60.7 %all_to_all.15.sent_ref = bf16[32,520,128]{2,1,0:T(8,128)(2,1)S(1)} all-to-all(bf16[32,520,128]{2,1,0:T(8,128)(2,1)S(1)} %apply_tiles.1), channel_id=1, replica_groups=mesh['xy'=16,'zl'=2,'quad'=4,'core'=2] {'xy','zl'}, dimensions={0} | all-to-all | bytes 8519680 | tf_op jit(solution)/shard_map/all_to_all | solution.py:207
  68.0 0.0 copy-done
  68.0 3.5 %join.1 = (f32[1024,128]{1,0:T(8,128)S(1)}, f32[1024,128]{1,0:T(8,128)S(1)}) custom-call(s32[2]{0:T(128)S(1)} %pad_add_fusion.spot_ref, bf16[24,128,512]{2,1,0:T(8,128)(2,1)S(1)} %bitcast.17, bf16[32,520,128]{2,1,0:T(8,128)(2,1)S(1)} %all_to_all.15.sent_ref), custom_call_target="tpu_custom_call" | custom-call | flops 2147483648 | bytes 9502720 | tf_op jit(solution)/shard_map/join/pallas_call | solution.py:171
  71.5 2.2 %collective-permute-start = (f32[1024,128]{1,0:T(8,128)S(1)}, f32[1024,128]{1,0:T(8,128)S(1)}, u32[]{:S(2)}, u32[]{:S(2)}) collective-permute-start(f32[1024,128]{1,0:T(8,128)S(1)} %get-tuple-element.12), channel_id=1, source_target_pairs={{0,1},{1,0},{2,3},{3,2},{4,5},{5,4},{6,7},{7,6},{8,9},{9,8},{10,11... | collective-permute-start | bytes 1572872 | tf_op jit(solution)/shard_map/ppermute | solution.py:209
  73.7 1.3 %gram_rows.1 = f32[1024,128]{1,0:T(8,128)S(1)} custom-call(s32[2]{0:T(128)S(1)} %pad_add_fusion.spot_ref, bf16[24,128,512]{2,1,0:T(8,128)(2,1)S(1)} %bitcast.18), custom_call_target="tpu_custom_call" | custom-call | flops 402653184 | bytes 1310720 | tf_op jit(solution)/shard_map/gram_rows/pallas_call | solution.py:118
  75.0 0.2 collective-permute-done
  75.2 0.1 add_add_fusion
  75.3 13.7 %all_to_all.16 = f32[16,64,128]{2,1,0:T(8,128)S(1)} all-to-all(f32[16,64,128]{2,1,0:T(8,128)S(1)} %bitcast.20), channel_id=1, replica_groups=mesh['xy'=16,'zl'=2,'quad'=4,'core'=2] {'xy'}, dimensions={0} | all-to-all | bytes 1048576 | tf_op jit(solution)/shard_map/all_to_all | solution.py:212
  89.1 13.7 %all_to_all.17 = f32[8,8,128]{2,1,0:T(8,128)S(1)} all-to-all(f32[8,8,128]{2,1,0:T(8,128)S(1)} %bitcast.21), channel_id=1, replica_groups=mesh['xy'=16,'zl'=2,'quad'=4,'core'=2] {'zl','quad'}, dimensions={0} | all-to-all | bytes 65536 | tf_op jit(solution)/shard_map/all_to_all | solution.py:213
  102.7 0.6 broadcast_multiply_fusion
  (2 shorter events, 0.0 us)
Async XLA Ops:
  7.3 60.7 %copy-start = (bf16[3072,512]{1,0:T(8,128)(2,1)S(1)}, bf16[3072,512]{1,0:T(8,128)(2,1)}, u32[]{:S(2)}) copy-start(bf16[3072,512]{1,0:T(8,128)(2,1)} %param.5) | copy-start | bytes 9437188
  71.5 3.7 %collective-permute-start = (f32[1024,128]{1,0:T(8,128)S(1)}, f32[1024,128]{1,0:T(8,128)S(1)}, u32[]{:S(2)}, u32[]{:S(2)}) collective-permute-start(f32[1024,128]{1,0:T(8,128)S(1)} %get-tuple-element.12), channel_id=1, source_target_pairs={{0,1},{1,0},{2,3},{3,2},{4,5},{5,4},{6,7},{7,6},{8,9},{9,8},{10,11... | collective-permute-start | bytes 1572872 | tf_op jit(solution)/shard_map/ppermute | solution.py:209
